TPU v7x, 32 devices: a whole 2x2x4 slice. The times are simulated.
32 devices in a mesh: trade: 2 (over y), date: 4 (over z), path: 4 (over x, core).
Axes of the slice: x: 2, y: 2, z: 4, core: 2. Of those that a mesh axis runs over, the one named last changes fastest.
Arguments:
- trade_values: bfloat16 [1280, 64, 512], P('trade', 'date', 'path'), parts along dimension 2, may hold values from -4 to 4
- set_of_trade: int32 [1280], P('trade'), may hold values from 0 to 255, as said below
- thresholds: float32 [256], replicated, may hold values from 0.2 to 2
- spreads: float32 [256], replicated, may hold values from 0.003 to 0.03
- retention: float32 [256, 64], replicated, may hold values from 0 to 1, as said below
Outputs:
- net_exposure: float32 [256, 64, 512], P('trade', 'date', 'path'), parts along dimension 2
- funding: float32 [256, 64, 512], P('trade', 'date', 'path'), parts along dimension 2
There are 4 independent parts, one for each index of `path`. A program takes and returns all parts, laid end to end along the dimension named above; an argument that names none is the same for every part. Nothing has to cross between parts.
Inputs may be any that keep to these rules, and one draw needn't show every extreme that they name: `set_of_trade`: trade n lies in trade block b = n // 640; it names a set of set block b (sets b * 128 to (b + 1) * 128 - 1) or of set block (b + 1) mod (2). The first 128 trades of block b name the sets of set block b in order. `retention`: strictly between 0 and 1.
All inputs are finite; a program needn't handle non-finite values.
Results may differ from a plain program's by a relative error of at most 0.0003.
Values sent between devices are 32-bit elements; how exact they have to be, the bound alone decides.
No kernel may reach another device: no remote copies, remote signals or barrier semaphores. Data moves between devices by JAX's collectives and lax.ppermute only.
A program may use at most 64 MiB of HBM per device.

v0:
```python
import jax
import jax.numpy as jnp
from jax import lax
from jax.sharding import PartitionSpec as P

LAG = 10


def from_behind(block, axis, distance):
    devices = range(lax.axis_size(axis))
    route = [((i - distance) % len(devices), i) for i in devices]
    return lax.ppermute(block, axis, route)


def shifted(value, axis, steps):
    count = lax.axis_size(axis)
    leading, last = (max(0, -steps), min(count, count - steps))
    return lax.ppermute(value, axis, [(source, source + steps) for source in range(leading, last)])


def entering(value, axis, join, neutral):
    count, mine = (lax.axis_size(axis), lax.axis_index(axis))
    pieces = jax.tree.map(lambda part: lax.all_gather(part, axis), value)
    total = jax.tree.map(
        lambda part, zero: jnp.full_like(part, 0) + jnp.asarray(zero, part.dtype), value, neutral
    )

    def step(position, total):
        longer = join(total, jax.tree.map(lambda part: part[position], pieces))
        return jax.tree.map(lambda new, old: jnp.where(position < mine, new, old), longer, total)

    return lax.fori_loop(0, count - 1, step, total)


def compose(earlier, later):
    return (earlier[0] * later[0], later[0] * earlier[1] + later[1])


def settle(sums, lagged, level, spread, rates):
    bound = level[:, None, None]
    collateral = jnp.maximum(lagged - bound, 0.0) - jnp.maximum(-lagged - bound, 0.0)
    exposure = sums - collateral
    costs = spread[:, None, None] * jnp.maximum(exposure, 0.0)
    cum_rate, local_funding = lax.associative_scan(compose, (rates[:, :, None], costs), axis=1)
    return (exposure, cum_rate, local_funding)


def combine_rows(labels, row_count, trade_values):
    rows = lax.broadcasted_iota(jnp.int32, (row_count, labels.shape[0]), 0)
    selector = (rows == labels[None, :]).astype(jnp.bfloat16)
    return jnp.einsum("sn,ntp->stp", selector, trade_values, preferred_element_type=jnp.float32)


def shards(trade_values, set_of_trade, thresholds, spreads, retention):
    set_count = thresholds.shape[0]
    dates_dev = trade_values.shape[1]
    paths = trade_values.shape[2]
    n_trade = lax.axis_size("trade")
    trade_pos = lax.axis_index("trade")
    date_pos = lax.axis_index("date")
    set_dev = set_count // n_trade
    first_set = trade_pos * set_dev
    offset = set_of_trade - first_set
    offset = jnp.where(offset < 0, offset + set_count, offset)
    nearby = combine_rows(offset, 2 * set_dev, trade_values)
    sums = nearby[:set_dev] + from_behind(nearby[set_dev:], "trade", 1)
    rim = shifted(sums[:, dates_dev - LAG :, :], "date", 1)
    lagged = jnp.concatenate([rim, sums[:, : dates_dev - LAG]], axis=1)
    level = lax.dynamic_slice_in_dim(thresholds, first_set, set_dev)
    spread = lax.dynamic_slice_in_dim(spreads, first_set, set_dev)
    rates = lax.dynamic_slice(retention, (first_set, date_pos * dates_dev), (set_dev, dates_dev))
    net_exposure, cum_rate, local_funding = settle(sums, lagged, level, spread, rates)
    identity = (jnp.ones((set_dev, 1), jnp.float32), jnp.zeros((set_dev, paths), jnp.float32))
    prefix = entering((cum_rate[:, -1, :], local_funding[:, -1, :]), "date", compose, identity)
    funding = local_funding + cum_rate * prefix[1][:, None, :]
    return (net_exposure, funding)


def solution(mesh):
    return jax.shard_map(
        shards,
        mesh=mesh,
        in_specs=(P("trade", "date", "path"), P("trade"), P(), P(), P()),
        out_specs=(P("trade", "date", "path"), P("trade", "date", "path")),
        check_vma=False,
    )
```

profile of v0, /device:TPU:0, one launch (start us, length us, event | category | flops | bytes accessed | tf_op | source)
XLA Modules:
  0.0 106.7 jit_solution(8493649848275835097)
XLA Ops:
  2.4 1.0 fusion.1
  3.4 1.3 %copy-done.1 = f32[256,16,128]{2,0,1:T(8,128)} copy-done((f32[256,16,128]{2,0,1:T(8,128)}, f32[256,16,128]{2,0,1:T(8,128)S(1)}, u32[]{:S(2)}) %copy-start.1) | copy-done | bytes 2097176
  4.7 1.0 slice.169
  5.8 3.0 %collective-permute-start = (f32[128,16,128]{2,0,1:T(8,128)}, f32[128,16,128]{2,0,1:T(8,128)}, u32[]{:S(2)}, u32[]{:S(2)}) collective-permute-start(f32[128,16,128]{2,0,1:T(8,128)} %slice.169), channel_id=1, source_target_pairs={{16,0},{0,16},{17,1},{1,17},{18,2},{2,18},{19,3},{3,19},{20,4},{4,... | collective-permute-start | bytes 3145736 | tf_op jit(solution)/shard_map/ppermute | solution.py:12
  9.9 22.4 %collective-permute-done = f32[128,16,128]{2,0,1:T(8,128)} collective-permute-done((f32[128,16,128]{2,0,1:T(8,128)}, f32[128,16,128]{2,0,1:T(8,128)}, u32[]{:S(2)}, u32[]{:S(2)}) %collective-permute-start) | collective-permute-done | bytes 1048608 | tf_op jit(solution)/shard_map/ppermute | solution.py:12
  32.2 1.7 %slice_add_fusion = f32[128,16,128]{2,0,1:T(8,128)S(1)} fusion(f32[128,16,128]{2,0,1:T(8,128)} %collective-permute-done, f32[256,16,128]{2,0,1:T(8,128)} %copy-done.1), kind=kLoop, calls=%fused_computation.5 | loop fusion | flops 262144 | bytes 3145728 | tf_op jit(solution)/shard_map/add | solution.py:66
  33.9 1.0 copy-done.2
  35.8 4.6 %collective-permute-start.1 = (f32[128,10,128]{2,0,1:T(8,128)}, f32[128,10,128]{2,0,1:T(8,128)}, u32[]{:S(2)}, u32[]{:S(2)}) collective-permute-start(f32[128,10,128]{2,0,1:T(8,128)} %slice.170), channel_id=1, source_target_pairs={{0,4},{4,8},{8,12},{1,5},{5,9},{9,13},{2,6},{6,10},{10,14},{3,7},{... | collective-permute-start | bytes 1966088 | tf_op jit(solution)/shard_map/ppermute | solution.py:18
  40.7 18.7 %all-gather = f32[512,1,1]{0,2,1:T(1,128)} all-gather(f32[128,1,1]{0,2,1:T(1,128)S(1)} %slice_add_fusion.6), channel_id=2, replica_groups=mesh['trade'=2,'date'=4,'path'=4] {'date'}, dimensions={0}, use_global_device_ids=true | all-gather | bytes 2560 | tf_op jit(solution)/shard_map/all_gather | solution.py:23
  59.4 1.0 slice.171
  60.4 1.8 %maximum_multiply_fusion = (f32[128,16,128]{2,0,1:T(8,128)S(1)}, f32[128,16,128]{2,0,1:T(8,128)S(1)}) fusion(f32[128]{0:T(128)S(1)} %dynamic_slice.24, f32[128,16,128]{2,0,1:T(8,128)} %copy-done.2, f32[128]{0:T(128)S(1)} %dynamic_slice.23, f32[128,6,128]{2,0,1:T(8,128)S(1)} %slice.171, f32[128,10,128]{2,0,1:T(8,128)} %collective-permute-done.1), kind=kLoop, calls=%fused_computation.8 | loop fusion | flops 2621440 | bytes 4195328 | tf_op jit(solution)/shard_map/mul | solution.py:43
  62.3 1.6 %copy.8 = f32[128,16,128]{2,1,0:T(8,128)} copy(f32[128,16,128]{2,0,1:T(8,128)S(1)} %get-tuple-element.128) | data formatting | bytes 2097152
  67.1 1.8 %pad.55 = f32[128,8,128]{2,0,1:T(8,128)S(1)} pad(f32[128,4,128]{2,0,1:T(8,128)} %add.137, f32[]{:T(128)} %constant.44.clone.1), padding=0_0_0x1_0_1x0_0_0 | pad | bytes 786436 | tf_op jit(solution)/shard_map/pad | solution.py:44
  68.9 1.1 %fusion.7 = f32[128,3,128]{2,0,1:T(8,128)S(1)} fusion(f32[128,4,128]{2,0,1:T(8,128)} %copy-done.6, f32[128,4,128]{2,0,1:T(8,128)S(1)} %pad.52, f32[128,8,128]{2,0,1:T(8,128)} %copy-done.4, f32[128,3]{0,1:T(4,128)S(1)} %bitcast.37), kind=kLoop, calls=%fused_computation.20 | loop fusion | flops 147456 | bytes 787968 | tf_op jit(solution)/shard_map/add | solution.py:36
  70.0 2.1 %pad.54 = f32[128,8,128]{2,0,1:T(8,128)} pad(f32[128,4,128]{2,0,1:T(8,128)S(1)} %pad_maximum_fusion.2, f32[]{:T(128)} %constant.44.clone.1), padding=0_0_0x0_1_1x0_0_0 | pad | bytes 786436 | tf_op jit(solution)/shard_map/pad | solution.py:44
  72.1 1.9 %add.139 = f32[128,8,128]{2,0,1:T(8,128)} add(f32[128,8,128]{2,0,1:T(8,128)} %pad.54, f32[128,8,128]{2,0,1:T(8,128)S(1)} %pad.55) | non-fusion elementwise | flops 131072 | bytes 1572864 | tf_op jit(solution)/shard_map/add | solution.py:44
  74.0 1.3 %fusion.5 = f32[128,7,128]{2,0,1:T(8,128)S(1)} fusion(f32[128,8,128]{2,0,1:T(8,128)S(1)} %pad.55, f32[128,8,128]{2,0,1:T(8,128)} %pad.54, f32[128,16,128]{2,0,1:T(8,128)} %copy-done.3, f32[128,7]{0,1:T(8,128)S(1)} %bitcast.35), kind=kLoop, calls=%fused_computation.15 | loop fusion | flops 344064 | bytes 1838592 | tf_op jit(solution)/shard_map/add | solution.py:36
  75.4 1.7 %pad_maximum_fusion.1 = f32[128,8,128]{2,0,1:T(8,128)} fusion(f32[128,7,128]{2,0,1:T(8,128)S(1)} %fusion.5, f32[128,1,128]{2,0,1:T(8,128)} %slice.172), kind=kLoop, calls=%fused_computation.12 | loop fusion | flops 131072 | bytes 1048576 | tf_op jit(solution)/shard_map/concatenate | solution.py:44
  77.1 5.7 %pad.56 = f32[128,16,128]{2,0,1:T(8,128)} pad(f32[128,8,128]{2,0,1:T(8,128)} %pad_maximum_fusion.1, f32[]{:T(128)} %constant.44.clone.1), padding=0_0_0x0_1_1x0_0_0 | pad | bytes 1572868 | tf_op jit(solution)/shard_map/pad | solution.py:44
  82.8 3.5 %pad.57 = f32[128,16,128]{2,0,1:T(8,128)} pad(f32[128,8,128]{2,0,1:T(8,128)S(1)} %copy-done.5, f32[]{:T(128)} %constant.44.clone.1), padding=0_0_0x1_0_1x0_0_0 | pad | bytes 1572868 | tf_op jit(solution)/shard_map/pad | solution.py:44
  87.2 13.8 %all-gather.1 = f32[512,1,128]{2,0,1:T(8,128)S(1)} all-gather(f32[128,1,128]{2,0,1:T(8,128)S(1)} %slice_add_fusion.4), channel_id=3, replica_groups=mesh['trade'=2,'date'=4,'path'=4] {'date'}, dimensions={0}, use_global_device_ids=true | all-gather | bytes 327680 | tf_op jit(solution)/shard_map/all_gather | solution.py:23
  101.0 2.2 %while.14 = (s32[]{:T(128)}, f32[128,128]{1,0:T(8,128)S(1)}, s32[]{:T(128)}, f32[4,128,1]{1,2,0:T(1,128)}, f32[4,128,128]{2,1,0:T(8,128)S(1)}, /*index=5*/s32[]{:T(128)}, s32[]{:T(128)}) while((s32[]{:T(128)}, f32[128,128]{1,0:T(8,128)S(1)}, s32[]{:T(128)}, f32[4,128,1]{1,2,0:T(1,128)}, f32[4,128,128]{2,1,0:T(8,128)S(1)}, ...), condition=%wide.region_1.2_spmd.clone, body=%wide.region_0.1_spmd.clone.sunk | while | flops 65540 | bytes 198257 | solution.py:32
  103.2 1.9 %multiply_add_fusion = f32[128,16,128]{2,0,1:T(8,128)S(1)} fusion(f32[128,16,128]{2,0,1:T(8,128)} %pad.56, f32[128,16,128]{2,0,1:T(8,128)} %pad.57, f32[128,128]{1,0:T(8,128)S(1)} %get-tuple-element.96, f32[128,16]{0,1:T(8,128)S(1)} %bitcast.34), kind=kLoop, calls=%fused_computation.7 | loop fusion | flops 786432 | bytes 3219456 | tf_op jit(solution)/shard_map/add | solution.py:75
  105.1 1.6 %copy.9 = f32[128,16,128]{2,1,0:T(8,128)} copy(f32[128,16,128]{2,0,1:T(8,128)S(1)} %multiply_add_fusion) | data formatting | bytes 2097152
  (69 shorter events, 10.3 us)
Async XLA Ops:
  0.6 1.8 %copy-start = (bf16[640,16,128]{2,1,0:T(8,128)(2,1)S(1)}, bf16[640,16,128]{2,1,0:T(8,128)(2,1)}, u32[]{:S(2)}) copy-start(bf16[640,16,128]{2,1,0:T(8,128)(2,1)} %param.7) | copy-start | bytes 7864324
  2.4 7.1 %copy-start.7 = (f32[256]{0:T(256)S(1)}, f32[256]{0:T(256)}, u32[]{:S(2)}) copy-start(f32[256]{0:T(256)} %param.10) | copy-start | bytes 3076
  2.4 7.2 %copy-start.8 = (f32[256]{0:T(256)S(1)}, f32[256]{0:T(256)}, u32[]{:S(2)}) copy-start(f32[256]{0:T(256)} %param.9) | copy-start | bytes 3076
  3.4 1.3 %copy-start.1 = (f32[256,16,128]{2,0,1:T(8,128)}, f32[256,16,128]{2,0,1:T(8,128)S(1)}, u32[]{:S(2)}) copy-start(f32[256,16,128]{2,0,1:T(8,128)S(1)} %fusion.1) | copy-start | bytes 6291460
  5.8 26.5 %collective-permute-start = (f32[128,16,128]{2,0,1:T(8,128)}, f32[128,16,128]{2,0,1:T(8,128)}, u32[]{:S(2)}, u32[]{:S(2)}) collective-permute-start(f32[128,16,128]{2,0,1:T(8,128)} %slice.169), channel_id=1, source_target_pairs={{16,0},{0,16},{17,1},{1,17},{18,2},{2,18},{19,3},{3,19},{20,4},{4,... | collective-permute-start | bytes 3145736 | tf_op jit(solution)/shard_map/ppermute | solution.py:12
  33.9 1.0 copy-start.2
  35.8 24.6 %collective-permute-start.1 = (f32[128,10,128]{2,0,1:T(8,128)}, f32[128,10,128]{2,0,1:T(8,128)}, u32[]{:S(2)}, u32[]{:S(2)}) collective-permute-start(f32[128,10,128]{2,0,1:T(8,128)} %slice.170), channel_id=1, source_target_pairs={{0,4},{4,8},{8,12},{1,5},{5,9},{9,13},{2,6},{6,10},{10,14},{3,7},{... | collective-permute-start | bytes 1966088 | tf_op jit(solution)/shard_map/ppermute | solution.py:18
  62.3 2.8 %copy-start.3 = (f32[128,16,128]{2,0,1:T(8,128)}, f32[128,16,128]{2,0,1:T(8,128)S(1)}, u32[]{:S(2)}) copy-start(f32[128,16,128]{2,0,1:T(8,128)S(1)} %get-tuple-element.127) | copy-start | bytes 3145732
  64.7 0.8 copy-start.4
  65.5 4.5 %slice-start = ((f32[128,8,128]{2,0,1:T(8,128)}), f32[128,1,128]{2,0,1:T(8,128)S(1)}, s32[]{:S(2)}) async-start(f32[128,8,128]{2,0,1:T(8,128)} %copy-done.4), calls=%async_computation | async-start | bytes 131072 | tf_op jit(solution)/shard_map/slice | solution.py:44
  65.7 0.7 copy-start.6
  75.4 7.4 %copy-start.5 = (f32[128,8,128]{2,0,1:T(8,128)S(1)}, f32[128,8,128]{2,0,1:T(8,128)}, u32[]{:S(2)}) copy-start(f32[128,8,128]{2,0,1:T(8,128)} %add.139) | copy-start | bytes 1572868
where the time goes:
time: 108 us; the launch traced here: 107 us
  blocking collectives  32.5 us (30%)
  local copies, waits for them, and re-layouts  27.3 us (25%)
  waiting for transfers between devices  22.4 us (21%)
  other arithmetic  14.9 us (14%)
  starting transfers between devices  7.56 us (7%)
    all_gather x2, blocking collectives, entering(): pieces = jax.tree.map(lambda part: lax.all_gather(part, axis), value)  32.5 us
    ppermute x1, waiting for transfers between devices, from_behind(): return lax.ppermute(block, axis, route)  22.4 us
    pad x12, local copies, waits for them, and re-layouts, settle(): lax.associative_scan(compose, (rates[:, :, None], costs), axis=1)  13.5 us
    unnamed x22, local copies, waits for them, and re-layouts  7.51 us
    ppermute x1, starting transfers between devices, shifted(): lax.ppermute(value, axis, [(source, source + steps) for source in range(l...  4.57 us
    add x9, other arithmetic, settle(): lax.associative_scan(compose, (rates[:, :, None], costs), axis=1)  3.55 us
    ppermute x1, starting transfers between devices, from_behind(): return lax.ppermute(block, axis, route)  3 us
    add x5, other arithmetic, compose(): return (earlier[0] * later[0], later[0] * earlier[1] + later[1])  2.91 us
  transfers between devices with their start and end apart: 2, of which 1 were waited for; matrix products, arithmetic and copies ran while one was open for 2% of the time, Pallas kernels for 0%

commit v1 on v0

v1 whole, which is shorter than its diff:
```python
import functools

import jax
import jax.numpy as jnp
from jax import lax
from jax.experimental import pallas as pl
from jax.experimental.pallas import tpu as pltpu
from jax.sharding import PartitionSpec as P

LAG = 10
GRANT = 12 * 1024 * 1024
RIM_PIECES = (3, 4, 3)


def shifted(value, axis, steps):
    count = lax.axis_size(axis)
    return lax.ppermute(value, axis, [(i, i + steps) for i in range(count - steps)])


def from_behind(value, axis):
    count = lax.axis_size(axis)
    return lax.ppermute(value, axis, [(i, (i + 1) % count) for i in range(count)])


def exchanged(value, axis, bit):
    count = lax.axis_size(axis)
    return lax.ppermute(value, axis, [(i, i ^ bit) for i in range(count) if i ^ bit < count])


def row_sums(labels, rows, values):
    place = lax.broadcasted_iota(jnp.int32, (rows, labels.shape[0]), 0)
    selector = (place == labels[None, :]).astype(jnp.bfloat16)
    return jnp.einsum("sn,ntp->tsp", selector, values, preferred_element_type=jnp.float32)


def whole(count):
    return [pl.BlockSpec(memory_space=pltpu.VMEM)] * count


def spread_kernel(at_ref, rates_ref, level_ref, spread_ref, rate_out, slab_out, level_out, spread_out):
    dates_dev, sets, paths = rate_out.shape
    slabs = slab_out.shape[0]
    across = (sets, paths)
    column = jnp.transpose(rates_ref[pl.ds(pl.multiple_of(at_ref[0], 8), dates_dev), :])
    for t in range(dates_dev):
        rate_out[t] = jnp.broadcast_to(column[:, t : t + 1], across)
    level_out[...] = jnp.broadcast_to(jnp.transpose(level_ref[...])[:, :1], across)
    spread_out[...] = jnp.broadcast_to(jnp.transpose(spread_ref[...])[:, :1], across)
    for d in range(slabs):
        total = rates_ref[d * dates_dev : d * dates_dev + 1, :]
        for t in range(1, dates_dev):
            total = total * rates_ref[d * dates_dev + t : d * dates_dev + t + 1, :]
        full = jnp.transpose(jnp.broadcast_to(total, (8, sets)))
        slab_out[d] = jnp.broadcast_to(full[:, :1], across)


def lay_across(date_start, rates, level, spread, dates_dev, paths):
    dates, sets = rates.shape
    slabs = dates // dates_dev
    f32 = jnp.float32
    shapes = [(dates_dev, sets, paths), (slabs, sets, paths), (sets, paths), (sets, paths)]
    return pl.pallas_call(
        spread_kernel,
        out_shape=[jax.ShapeDtypeStruct(s, f32) for s in shapes],
        in_specs=[pl.BlockSpec(memory_space=pltpu.SMEM)] + whole(3),
        out_specs=whole(4),
        compiler_params=pltpu.CompilerParams(vmem_limit_bytes=GRANT),
        name="lay_across",
    )(date_start, rates, jnp.broadcast_to(level, (8, sets)), jnp.broadcast_to(spread, (8, sets)))


def gather_dates(refs):
    return [(ref, i) for ref in refs for i in range(ref.shape[0])]


def cost_kernel(split, *refs):
    early, late, rims, level_ref, spread_ref, rate_ref, cost_out, last_out = unpack(split, refs)
    sums = early + late
    sets, paths = level_ref.shape
    block = 32

    def body(j, _):
        rows = pl.ds(pl.multiple_of(j * block, block), block)
        level, spread = level_ref[rows, :], spread_ref[rows, :]
        held = []
        state = jnp.zeros((block, paths), jnp.float32)
        for t in range(len(sums)):
            now = sums[t](rows)
            held.append(now)
            lagged = rims[t](rows) if t < LAG else held[t - LAG]
            exposure = net(now, lagged, level)
            cost = spread * jnp.maximum(exposure, 0.0)
            cost_out[t, rows, :] = cost
            state = rate_ref[t, rows, :] * state + cost
        last_out[rows, :] = state
        return 0

    lax.fori_loop(0, sets // block, body, 0)


def exposure_kernel(split, *refs):
    early, late, rims, level_ref, out = unpack(split, refs)
    sums = early + late
    sets, paths = level_ref.shape
    dates_dev = len(sums)
    block = 32

    def body(j, _):
        start = pl.multiple_of(j * block, block)
        rows = pl.ds(start, block)
        level = level_ref[rows, :]
        held = []
        for t in range(dates_dev):
            now = sums[t](rows)
            held.append(now)
            lagged = rims[t](rows) if t < LAG else held[t - LAG]
            out[pl.ds(start * dates_dev + t, block, stride=dates_dev), :] = net(now, lagged, level)
        return 0

    lax.fori_loop(0, sets // block, body, 0)


def net(now, lagged, level):
    return now - (jnp.maximum(lagged - level, 0.0) - jnp.maximum(-lagged - level, 0.0))


def unpack(split, refs):
    rim_count, early_dates = split
    own_ref, other_ref = refs[:2]
    late_refs = refs[2 : 2 + rim_count]
    rim_refs = refs[2 + rim_count : 2 + 2 * rim_count]

    def added(t):
        return lambda rows: own_ref[t, rows, :] + other_ref[t, rows, :]

    def plain(ref, i):
        return lambda rows: ref[i, rows, :]

    early = [added(t) for t in range(early_dates)]
    late = [plain(ref, i) for ref, i in gather_dates(late_refs)]
    rims = [plain(ref, i) for ref, i in gather_dates(rim_refs)]
    return (early, late, rims, *refs[2 + 2 * rim_count :])


def funding_kernel(carry_ref, cost_ref, rate_ref, out):
    dates_dev, sets, paths = cost_ref.shape
    block = 32

    def body(j, _):
        start = pl.multiple_of(j * block, block)
        rows = pl.ds(start, block)
        state = carry_ref[rows, :]
        for t in range(dates_dev):
            state = rate_ref[t, rows, :] * state + cost_ref[t, rows, :]
            out[pl.ds(start * dates_dev + t, block, stride=dates_dev), :] = state
        return 0

    lax.fori_loop(0, sets // block, body, 0)


def carry_in(last, slab_rates, axis):
    count, mine = lax.axis_size(axis), lax.axis_index(axis)
    entering = jnp.zeros_like(last)
    group, before = last, jnp.ones_like(last)
    group_rate = lax.dynamic_index_in_dim(slab_rates, mine, 0, keepdims=False)
    bit = 1
    while bit < count:
        other = exchanged(group, axis, bit)
        upper = (mine & bit) != 0
        if 2 * bit < count:
            base = (mine // (2 * bit)) * (2 * bit) + bit
            upper_rate = functools.reduce(
                jnp.multiply,
                [lax.dynamic_index_in_dim(slab_rates, base + i, 0, keepdims=False) for i in range(bit)],
            )
        entering = jnp.where(upper, entering + before * other, entering)
        if 2 * bit < count:
            base = (mine // (2 * bit)) * (2 * bit)
            lower_rate = functools.reduce(
                jnp.multiply,
                [lax.dynamic_index_in_dim(slab_rates, base + i, 0, keepdims=False) for i in range(bit)],
            )
            group = jnp.where(upper, group + upper_rate * other, other + upper_rate * group)
            before = jnp.where(upper, before * lower_rate, before)
        bit *= 2
    return entering


def shards(trade_values, set_of_trade, thresholds, spreads, retention):
    set_count = thresholds.shape[0]
    dates_dev, paths = trade_values.shape[1:]
    trade_pos, date_pos = lax.axis_index("trade"), lax.axis_index("date")
    sets = set_count // lax.axis_size("trade")
    first_set = trade_pos * sets
    offset = set_of_trade - first_set
    offset = jnp.where(offset < 0, offset + set_count, offset)
    early_dates = dates_dev - LAG

    f32 = jnp.float32
    bounds = [early_dates]
    for size in RIM_PIECES:
        bounds.append(bounds[-1] + size)
    spans = list(zip(bounds[:-1], bounds[1:]))

    def arriving(span):
        part = row_sums(offset - sets, sets, trade_values[:, span[0] : span[1]])
        return from_behind(part, "trade")

    own = row_sums(offset, sets, trade_values)
    late, rims = [], []
    for span in spans:
        sums = own[span[0] : span[1]] + arriving(span)
        late.append(sums)
        rims.append(shifted(sums, "date", 1))
    other = arriving((0, early_dates))

    level = lax.dynamic_slice_in_dim(thresholds, first_set, sets)
    spread = lax.dynamic_slice_in_dim(spreads, first_set, sets)
    rates = lax.dynamic_slice_in_dim(retention.T, first_set, sets, 1)
    date_start = (date_pos * dates_dev)[None].astype(jnp.int32)
    rate_all, slab_rates, level_all, spread_all = lay_across(
        date_start, rates, level, spread, dates_dev, paths
    )

    split = (len(spans), early_dates)
    flat = jax.ShapeDtypeStruct((sets * dates_dev, paths), f32)
    tall = jax.ShapeDtypeStruct((dates_dev, sets, paths), f32)
    parts = (own, other, *late, *rims)
    costs, last = pl.pallas_call(
        functools.partial(cost_kernel, split),
        out_shape=[tall, jax.ShapeDtypeStruct((sets, paths), f32)],
        in_specs=whole(len(parts) + 3),
        out_specs=whole(2),
        compiler_params=pltpu.CompilerParams(vmem_limit_bytes=GRANT),
        name="costs",
    )(*parts, level_all, spread_all, rate_all)
    net_exposure = pl.pallas_call(
        functools.partial(exposure_kernel, split),
        out_shape=flat,
        in_specs=whole(len(parts) + 1),
        out_specs=pl.BlockSpec(memory_space=pltpu.VMEM),
        compiler_params=pltpu.CompilerParams(vmem_limit_bytes=GRANT),
        name="exposure",
    )(*parts, level_all)
    carry = carry_in(last, slab_rates, "date")
    funding = pl.pallas_call(
        funding_kernel,
        out_shape=flat,
        in_specs=whole(3),
        out_specs=pl.BlockSpec(memory_space=pltpu.VMEM),
        compiler_params=pltpu.CompilerParams(vmem_limit_bytes=GRANT),
        name="funding",
    )(carry, costs, rate_all)
    shape = (sets, dates_dev, paths)
    return net_exposure.reshape(shape), funding.reshape(shape)


def solution(mesh):
    return jax.shard_map(
        shards,
        mesh=mesh,
        in_specs=(P("trade", "date", "path"), P("trade"), P(), P(), P()),
        out_specs=(P("trade", "date", "path"), P("trade", "date", "path")),
        check_vma=False,
    )
```

time: 108 us -> 68.5 us (0.63)
  blocking collectives: 32.5 us -> 0 us
  local copies, waits for them, and re-layouts: 27.3 us -> 5.8 us
  starting transfers between devices: 7.56 us -> 22.2 us
  other arithmetic: 14.9 us -> 2.52 us
  Pallas kernels: 0 us -> 6.81 us
  matrix products: 1 us -> 6.95 us
    all_gather x2 -> x0, blocking collectives: 32.5 us -> none  [entering(): pieces = jax.tree.map(lambda part: lax.all_gather(part, axis), value)]
    ppermute x2 -> x9, starting transfers between devices: 7.56 us -> 22.2 us  [the longest x3 11.4 us: shifted(): lax.ppermute(value, axis, [(i, i + steps) for i in range(count - steps)])]
    pad x12 -> x0, local copies, waits for them, and re-layouts: 13.5 us -> none  [settle(): lax.associative_scan(compose, (rates[:, :, None], costs), axis=1)]
    add x16 -> x2, other arithmetic: 10 us -> 0.08 us  [shards(): sums = own[span[0]:span[1]] + arriving(span)]
    pallas_call x0 -> x4, Pallas kernels: none -> 6.81 us  [the longest x1 2.62 us: shards(): pl.pallas_call(functools.partial(exposure_kernel, split), out_shape=flat,...]
    dot_general x1 -> x5, matrix products: 1 us -> 6.95 us  [row_sums(): jnp.einsum('sn,ntp->tsp', selector, values, preferred_element_type=jnp.fl...]
    slice x8 -> x0, local copies, waits for them, and re-layouts: 3.58 us -> none  [the longest x1 1.04 us: shards(): sums = nearby[:set_dev] + from_behind(nearby[set_dev:], 'trade', 1)]
    mul x3 -> x0, local copies, waits for them, and re-layouts: 1.9 us -> none  [compose(): return (earlier[0] * later[0], later[0] * earlier[1] + later[1])]
  transfers between devices with their start and end apart: 2 -> 9, of which waited for: 1 -> 4; matrix products, arithmetic and copies ran while one was open for 2% -> 7% of each run, Pallas kernels for 0% -> 5%
where the time goes in v1:
time: 68.5 us; the launch traced here: 68 us
  waiting for transfers between devices  22.9 us (33%)
  starting transfers between devices  22.2 us (32%)
  matrix products  6.95 us (10%)
  Pallas kernels  6.81 us (10%)
  local copies, waits for them, and re-layouts  5.8 us (8%)
  other arithmetic  2.52 us (4%)
  between operations  0.78 us (1%)
    ppermute x4, waiting for transfers between devices, from_behind(): lax.ppermute(value, axis, [(i, (i + 1) % count) for i in range(count)])  16.5 us
    ppermute x3, starting transfers between devices, shifted(): lax.ppermute(value, axis, [(i, i + steps) for i in range(count - steps)])  11.4 us
    dot_general x5, matrix products, row_sums(): jnp.einsum('sn,ntp->tsp', selector, values, preferred_element_type=jnp.fl...  6.95 us
    unnamed x17, local copies, waits for them, and re-layouts  5.65 us
    ppermute x2, starting transfers between devices, exchanged(): lax.ppermute(value, axis, [(i, i ^ bit) for i in range(count) if i ^ bit...  5.62 us
    ppermute x4, starting transfers between devices, from_behind(): lax.ppermute(value, axis, [(i, (i + 1) % count) for i in range(count)])  5.22 us
    ppermute x3, waiting for transfers between devices, shifted(): lax.ppermute(value, axis, [(i, i + steps) for i in range(count - steps)])  3.83 us
    pallas_call x1, Pallas kernels, shards(): pl.pallas_call(functools.partial(exposure_kernel, split), out_shape=flat,...  2.62 us
  transfers between devices with their start and end apart: 9, of which 4 were waited for; matrix products, arithmetic and copies ran while one was open for 7% of the time, Pallas kernels for 5%

profile of v1, /device:TPU:0, one launch (start us, length us, event | category | flops | bytes accessed | tf_op | source)
XLA Modules:
  0.0 68.0 jit_solution(16857674756613254096)
XLA Ops:
  0.7 3.9 %copy.7 = bf16[640,16,128]{2,0,1:T(8,128)(2,1)} copy(bf16[640,16,128]{2,1,0:T(8,128)(2,1)} %param.5) | data formatting | bytes 5242880 | tf_op args[0]
  4.6 2.4 %convolution_bitcast_fusion.1 = f32[6,128,128]{2,1,0:T(8,128)} fusion(bf16[640,16,128]{2,0,1:T(8,128)(2,1)} %copy.7, s32[640]{0:T(1024)S(1)} %get-tuple-element.14), kind=kOutput, calls=%fused_computation.1 | convolution fusion | flops 125911040 | bytes 1378816 | tf_op jit(solution)/shard_map/sn,ntp->tsp/dot_general | solution.py:33
  7.0 3.0 %collective-permute-start = (f32[6,128,128]{2,1,0:T(8,128)}, f32[6,128,128]{2,1,0:T(8,128)S(1)}, u32[]{:S(2)}, u32[]{:S(2)}) collective-permute-start(f32[6,128,128]{2,1,0:T(8,128)} %convolution_bitcast_fusion.1), channel_id=1, source_target_pairs={{0,16},{16,0},{1,17},{17,1},{2,18},{18,2},{3,19},{19,3},{4,20},{20... | collective-permute-start | bytes 1179656 | tf_op jit(solution)/shard_map/ppermute | solution.py:22
  10.0 1.3 %convolution_bitcast_fusion.3 = f32[3,128,128]{2,1,0:T(8,128)S(1)} fusion(bf16[640,16,128]{2,0,1:T(8,128)(2,1)} %copy.7, s32[640]{0:T(1024)S(1)} %get-tuple-element.14), kind=kOutput, calls=%fused_computation.3 | convolution fusion | flops 62996480 | bytes 690688 | tf_op jit(solution)/shard_map/sn,ntp->tsp/dot_general | solution.py:33
  11.4 1.3 %convolution_bitcast_fusion.4 = f32[3,128,128]{2,1,0:T(8,128)S(1)} fusion(bf16[640,16,128]{2,0,1:T(8,128)(2,1)} %copy.7, s32[640]{0:T(1024)S(1)} %get-tuple-element.14), kind=kOutput, calls=%fused_computation.4 | convolution fusion | flops 62996480 | bytes 690688 | tf_op jit(solution)/shard_map/sn,ntp->tsp/dot_general | solution.py:33
  12.7 2.1 %collective-permute-start.1 = (f32[3,128,128]{2,1,0:T(8,128)S(1)}, f32[3,128,128]{2,1,0:T(8,128)S(1)}, u32[]{:S(2)}, u32[]{:S(2)}) collective-permute-start(f32[3,128,128]{2,1,0:T(8,128)S(1)} %convolution_bitcast_fusion.4), channel_id=1, source_target_pairs={{0,16},{16,0},{1,17},{17,1},{2,18},{18,2},{3,19},{19,3},{4,20},{20... | collective-permute-start | bytes 589832 | tf_op jit(solution)/shard_map/ppermute | solution.py:22
  14.7 1.4 %convolution_bitcast_fusion.2 = f32[4,128,128]{2,1,0:T(8,128)S(1)} fusion(bf16[640,16,128]{2,0,1:T(8,128)(2,1)} %copy.7, s32[640]{0:T(1024)S(1)} %get-tuple-element.14), kind=kOutput, calls=%fused_computation.2 | convolution fusion | flops 83968000 | bytes 920064 | tf_op jit(solution)/shard_map/sn,ntp->tsp/dot_general | solution.py:33
  16.9 16.5 %collective-permute-done.2 = f32[4,128,128]{2,1,0:T(8,128)S(1)} collective-permute-done((f32[4,128,128]{2,1,0:T(8,128)S(1)}, f32[4,128,128]{2,1,0:T(8,128)S(1)}, u32[]{:S(2)}, u32[]{:S(2)}) %collective-permute-start.2) | collective-permute-done | bytes 262176 | tf_op jit(solution)/shard_map/ppermute | solution.py:22
  33.4 3.7 %collective-permute-start.5 = (f32[4,128,128]{2,1,0:T(8,128)S(1)}, f32[4,128,128]{2,1,0:T(8,128)S(1)}, u32[]{:S(2)}, u32[]{:S(2)}) collective-permute-start(f32[4,128,128]{2,1,0:T(8,128)S(1)} %slice_add_fusion.refs_3_), channel_id=1, source_target_pairs={{0,4},{4,8},{8,12},{1,5},{5,9},{9,13},{2,6},{6,10},{10,14},{3,7},{... | collective-permute-start | bytes 786440 | tf_op jit(solution)/shard_map/ppermute | solution.py:17
  37.2 4.1 %collective-permute-start.4 = (f32[3,128,128]{2,1,0:T(8,128)S(1)}, f32[3,128,128]{2,1,0:T(8,128)}, u32[]{:S(2)}, u32[]{:S(2)}) collective-permute-start(f32[3,128,128]{2,1,0:T(8,128)S(1)} %get-tuple-element.17.refs_2_), channel_id=1, source_target_pairs={{0,4},{4,8},{8,12},{1,5},{5,9},{9,13},{2,6},{6,10},{10,14},{3,7},{... | collective-permute-start | bytes 589832 | tf_op jit(solution)/shard_map/ppermute | solution.py:17
  41.4 3.5 %collective-permute-start.6 = (f32[3,128,128]{2,1,0:T(8,128)S(1)}, f32[3,128,128]{2,1,0:T(8,128)}, u32[]{:S(2)}, u32[]{:S(2)}) collective-permute-start(f32[3,128,128]{2,1,0:T(8,128)S(1)} %get-tuple-element.16.refs_4_), channel_id=1, source_target_pairs={{0,4},{4,8},{8,12},{1,5},{5,9},{9,13},{2,6},{6,10},{10,14},{3,7},{... | collective-permute-start | bytes 589832 | tf_op jit(solution)/shard_map/ppermute | solution.py:17
  45.1 0.7 lay_across.1
  45.7 0.7 %copy-done.3 = f32[4,128,128]{2,1,0:T(8,128)} copy-done((f32[4,128,128]{2,1,0:T(8,128)}, f32[4,128,128]{2,1,0:T(8,128)S(1)}, u32[]{:S(2)}) %copy-start.3) | copy-done | bytes 262168
  46.4 1.6 %collective-permute-done.4.refs_5_ = f32[3,128,128]{2,1,0:T(8,128)} collective-permute-done((f32[3,128,128]{2,1,0:T(8,128)S(1)}, f32[3,128,128]{2,1,0:T(8,128)}, u32[]{:S(2)}, u32[]{:S(2)}) %collective-permute-start.4) | collective-permute-done | bytes 196640 | tf_op jit(solution)/shard_map/ppermute | solution.py:17
  48.0 2.2 %collective-permute-done.6.refs_7_ = f32[3,128,128]{2,1,0:T(8,128)} collective-permute-done((f32[3,128,128]{2,1,0:T(8,128)S(1)}, f32[3,128,128]{2,1,0:T(8,128)}, u32[]{:S(2)}, u32[]{:S(2)}) %collective-permute-start.6) | collective-permute-done | bytes 196640 | tf_op jit(solution)/shard_map/ppermute | solution.py:17
  50.3 2.1 %costs.1 = (f32[16,128,128]{2,1,0:T(8,128)S(1)}, f32[128,128]{1,0:T(8,128)}) custom-call(f32[16,128,128]{2,1,0:T(8,128)S(1)} %convolution_bitcast_fusion.refs_0_, f32[6,128,128]{2,1,0:T(8,128)S(1)} %collective-permute-done.refs_1_, f32[3,128,128]{2,1,0:T(8,128)S(1)} %get-tuple-element.17.refs_2_, f32[4,128,128]{2,1,0:T(8,128)S(1)} %slice_add_fusion.refs_3_, ...), custom_call_target="tpu_custom_call" | custom-call | tf_op jit(solution)/shard_map/costs/pallas_call | solution.py:229
  52.3 1.0 %copy-done.1 = f32[16,128,128]{2,1,0:T(8,128)} copy-done((f32[16,128,128]{2,1,0:T(8,128)}, f32[16,128,128]{2,1,0:T(8,128)S(1)}, u32[]{:S(2)}) %copy-start.1) | copy-done | bytes 1048600
  53.3 2.6 %collective-permute-start.7 = (f32[128,128]{1,0:T(8,128)}, f32[128,128]{1,0:T(8,128)}, u32[]{:S(2)}, u32[]{:S(2)}) collective-permute-start(f32[128,128]{1,0:T(8,128)} %get-tuple-element.11), channel_id=1, source_target_pairs={{0,4},{4,0},{8,12},{12,8},{1,5},{5,1},{9,13},{13,9},{2,6},{6,2},{1... | collective-permute-start | bytes 196616 | tf_op jit(solution)/shard_map/ppermute | solution.py:27
  55.9 2.6 %collective-permute-done.7 = f32[128,128]{1,0:T(8,128)} collective-permute-done((f32[128,128]{1,0:T(8,128)}, f32[128,128]{1,0:T(8,128)}, u32[]{:S(2)}, u32[]{:S(2)}) %collective-permute-start.7) | collective-permute-done | bytes 65568 | tf_op jit(solution)/shard_map/ppermute | solution.py:27
  58.4 1.5 %fusion.17 = f32[128,128]{1,0:T(8,128)} fusion(f32[128,128]{1,0:T(8,128)} %get-tuple-element.11, f32[128,128]{1,0:T(8,128)} %collective-permute-done.7, f32[4,128,128]{2,1,0:T(8,128)} %copy-done.3, s32[]{:T(128)S(6)} %select_n.59, pred[]{:T(512)S(6)} %ne.17), kind=kLoop, calls=%fused_computation.25 | loop fusion | flops 81920 | bytes 262149 | tf_op jit(solution)/shard_map/jit(_where)/select_n | solution.py:183
  60.0 3.0 %collective-permute-start.8 = (f32[128,128]{1,0:T(8,128)}, f32[128,128]{1,0:T(8,128)}, u32[]{:S(2)}, u32[]{:S(2)}) collective-permute-start(f32[128,128]{1,0:T(8,128)} %fusion.17), channel_id=1, source_target_pairs={{0,8},{4,12},{8,0},{12,4},{1,9},{5,13},{9,1},{13,5},{2,10},{6,14},... | collective-permute-start | bytes 196616 | tf_op jit(solution)/shard_map/ppermute | solution.py:27
  63.0 2.6 %exposure.1 = f32[2048,128]{1,0:T(8,128)} custom-call(f32[16,128,128]{2,1,0:T(8,128)S(1)} %convolution_bitcast_fusion.refs_0_, f32[6,128,128]{2,1,0:T(8,128)S(1)} %collective-permute-done.refs_1_, f32[3,128,128]{2,1,0:T(8,128)S(1)} %get-tuple-element.17.refs_2_, f32[4,128,128]{2,1,0:T(8,128)S(1)} %slice_add_fusion.refs_3_, ...), custom_call_target="tpu_custom_call" | custom-call | tf_op jit(solution)/shard_map/exposure/pallas_call | solution.py:237
  65.6 0.9 %add_select_fusion.carry_ref = f32[128,128]{1,0:T(8,128)S(1)} fusion(f32[128,128]{1,0:T(8,128)} %collective-permute-done.8, f32[4,128,128]{2,1,0:T(8,128)} %copy-done.3, s32[]{:T(128)S(6)} %select_n.56, f32[128,128]{1,0:T(8,128)} %collective-permute-done.7, pred[]{:T(512)S(6)} %ne.17, pred[]{:T(512)S(6)} %ne.16), kind=kLoop, calls=%fused_computation.21 | loop fusion | flops 81920 | bytes 264192 | tf_op jit(solution)/shard_map/jit(_where)/select_n | solution.py:176
  66.5 1.5 %funding.1 = f32[2048,128]{1,0:T(8,128)} custom-call(f32[128,128]{1,0:T(8,128)S(1)} %add_select_fusion.carry_ref, f32[16,128,128]{2,1,0:T(8,128)S(1)} %copy-done.2, f32[16,128,128]{2,1,0:T(8,128)S(1)} %get-tuple-element.10.refs_10_.rate_ref), custom_call_target="tpu_custom_call" | custom-call | tf_op jit(solution)/shard_map/funding/pallas_call | solution.py:246
  (30 shorter events, 1.1 us)
Async XLA Ops:
  0.6 44.4 %copy-start = (f32[256,64]{0,1:T(8,128)S(1)}, f32[256,64]{0,1:T(8,128)}, u32[]{:S(2)}) copy-start(f32[256,64]{0,1:T(8,128)} %param.9) | copy-start | bytes 196612
  0.7 4.0 %copy-start.5 = (s32[640]{0:T(1024)S(1)}, s32[640]{0:T(1024)}, u32[]{:S(2)}) copy-start(s32[640]{0:T(1024)} %param.6) | copy-start | bytes 7684
  4.6 11.6 %copy-start.4 = (bf16[640,16,128]{2,1,0:T(8,128)(2,1)S(1)}, bf16[640,16,128]{2,1,0:T(8,128)(2,1)}, u32[]{:S(2)}) copy-start(bf16[640,16,128]{2,1,0:T(8,128)(2,1)} %param.5) | copy-start | bytes 7864324
  7.0 39.4 %collective-permute-start = (f32[6,128,128]{2,1,0:T(8,128)}, f32[6,128,128]{2,1,0:T(8,128)S(1)}, u32[]{:S(2)}, u32[]{:S(2)}) collective-permute-start(f32[6,128,128]{2,1,0:T(8,128)} %convolution_bitcast_fusion.1), channel_id=1, source_target_pairs={{0,16},{16,0},{1,17},{17,1},{2,18},{18,2},{3,19},{19,3},{4,20},{20... | collective-permute-start | bytes 1179656 | tf_op jit(solution)/shard_map/ppermute | solution.py:22
  11.3 25.8 %collective-permute-start.3 = (f32[3,128,128]{2,1,0:T(8,128)S(1)}, f32[3,128,128]{2,1,0:T(8,128)S(1)}, u32[]{:S(2)}, u32[]{:S(2)}) collective-permute-start(f32[3,128,128]{2,1,0:T(8,128)S(1)} %convolution_bitcast_fusion.3), channel_id=1, source_target_pairs={{0,16},{16,0},{1,17},{17,1},{2,18},{18,2},{3,19},{19,3},{4,20},{20... | collective-permute-start | bytes 589832 | tf_op jit(solution)/shard_map/ppermute | solution.py:22
  12.7 24.5 %collective-permute-start.1 = (f32[3,128,128]{2,1,0:T(8,128)S(1)}, f32[3,128,128]{2,1,0:T(8,128)S(1)}, u32[]{:S(2)}, u32[]{:S(2)}) collective-permute-start(f32[3,128,128]{2,1,0:T(8,128)S(1)} %convolution_bitcast_fusion.4), channel_id=1, source_target_pairs={{0,16},{16,0},{1,17},{17,1},{2,18},{18,2},{3,19},{19,3},{4,20},{20... | collective-permute-start | bytes 589832 | tf_op jit(solution)/shard_map/ppermute | solution.py:22
  16.1 17.3 %collective-permute-start.2 = (f32[4,128,128]{2,1,0:T(8,128)S(1)}, f32[4,128,128]{2,1,0:T(8,128)S(1)}, u32[]{:S(2)}, u32[]{:S(2)}) collective-permute-start(f32[4,128,128]{2,1,0:T(8,128)S(1)} %convolution_bitcast_fusion.2), channel_id=1, source_target_pairs={{0,16},{16,0},{1,17},{17,1},{2,18},{18,2},{3,19},{19,3},{4,20},{20... | collective-permute-start | bytes 786440 | tf_op jit(solution)/shard_map/ppermute | solution.py:22
  16.2 28.7 %copy-start.6 = (f32[256]{0:T(256)S(1)}, f32[256]{0:T(256)}, u32[]{:S(2)}) copy-start(f32[256]{0:T(256)} %param.7) | copy-start | bytes 3076
  16.2 28.7 %copy-start.7 = (f32[256]{0:T(256)S(1)}, f32[256]{0:T(256)}, u32[]{:S(2)}) copy-start(f32[256]{0:T(256)} %param.8) | copy-start | bytes 3076
  33.4 16.8 %collective-permute-start.5 = (f32[4,128,128]{2,1,0:T(8,128)S(1)}, f32[4,128,128]{2,1,0:T(8,128)S(1)}, u32[]{:S(2)}, u32[]{:S(2)}) collective-permute-start(f32[4,128,128]{2,1,0:T(8,128)S(1)} %slice_add_fusion.refs_3_), channel_id=1, source_target_pairs={{0,4},{4,8},{8,12},{1,5},{5,9},{9,13},{2,6},{6,10},{10,14},{3,7},{... | collective-permute-start | bytes 786440 | tf_op jit(solution)/shard_map/ppermute | solution.py:17
  37.2 10.8 %collective-permute-start.4 = (f32[3,128,128]{2,1,0:T(8,128)S(1)}, f32[3,128,128]{2,1,0:T(8,128)}, u32[]{:S(2)}, u32[]{:S(2)}) collective-permute-start(f32[3,128,128]{2,1,0:T(8,128)S(1)} %get-tuple-element.17.refs_2_), channel_id=1, source_target_pairs={{0,4},{4,8},{8,12},{1,5},{5,9},{9,13},{2,6},{6,10},{10,14},{3,7},{... | collective-permute-start | bytes 589832 | tf_op jit(solution)/shard_map/ppermute | solution.py:17
  41.4 8.9 %collective-permute-start.6 = (f32[3,128,128]{2,1,0:T(8,128)S(1)}, f32[3,128,128]{2,1,0:T(8,128)}, u32[]{:S(2)}, u32[]{:S(2)}) collective-permute-start(f32[3,128,128]{2,1,0:T(8,128)S(1)} %get-tuple-element.16.refs_4_), channel_id=1, source_target_pairs={{0,4},{4,8},{8,12},{1,5},{5,9},{9,13},{2,6},{6,10},{10,14},{3,7},{... | collective-permute-start | bytes 589832 | tf_op jit(solution)/shard_map/ppermute | solution.py:17
  45.7 0.7 %copy-start.3 = (f32[4,128,128]{2,1,0:T(8,128)}, f32[4,128,128]{2,1,0:T(8,128)S(1)}, u32[]{:S(2)}) copy-start(f32[4,128,128]{2,1,0:T(8,128)S(1)} %get-tuple-element.12) | copy-start | bytes 786436
  52.3 1.0 %copy-start.1 = (f32[16,128,128]{2,1,0:T(8,128)}, f32[16,128,128]{2,1,0:T(8,128)S(1)}, u32[]{:S(2)}) copy-start(f32[16,128,128]{2,1,0:T(8,128)S(1)} %get-tuple-element.13.cost_ref) | copy-start | bytes 3145732
  53.3 5.1 %collective-permute-start.7 = (f32[128,128]{1,0:T(8,128)}, f32[128,128]{1,0:T(8,128)}, u32[]{:S(2)}, u32[]{:S(2)}) collective-permute-start(f32[128,128]{1,0:T(8,128)} %get-tuple-element.11), channel_id=1, source_target_pairs={{0,4},{4,0},{8,12},{12,8},{1,5},{5,1},{9,13},{13,9},{2,6},{6,2},{1... | collective-permute-start | bytes 196616 | tf_op jit(solution)/shard_map/ppermute | solution.py:27
  60.0 5.7 %collective-permute-start.8 = (f32[128,128]{1,0:T(8,128)}, f32[128,128]{1,0:T(8,128)}, u32[]{:S(2)}, u32[]{:S(2)}) collective-permute-start(f32[128,128]{1,0:T(8,128)} %fusion.17), channel_id=1, source_target_pairs={{0,8},{4,12},{8,0},{12,4},{1,9},{5,13},{9,1},{13,5},{2,10},{6,14},... | collective-permute-start | bytes 196616 | tf_op jit(solution)/shard_map/ppermute | solution.py:27
  63.0 3.5 %copy-start.2 = (f32[16,128,128]{2,1,0:T(8,128)S(1)}, f32[16,128,128]{2,1,0:T(8,128)}, u32[]{:S(2)}) copy-start(f32[16,128,128]{2,1,0:T(8,128)} %copy-done.1) | copy-start | bytes 3145732

commit v2 on v0

v2 whole, which is shorter than its diff:
```python
import functools

import jax
import jax.numpy as jnp
from jax import lax
from jax.experimental import pallas as pl
from jax.experimental.pallas import tpu as pltpu
from jax.sharding import PartitionSpec as P


LAG = 10
GRANT = 8 * 1024 * 1024
RIM_PIECES = (3, 3, 4)
BLOCK = 32


def ahead(value, axis):
    count = lax.axis_size(axis)
    return lax.ppermute(value, axis, [(i, (i + 1) % count) for i in range(count)])


def exchanged(value, axis, bit):
    return lax.ppermute(value, axis, [(i, i ^ bit) for i in range(lax.axis_size(axis))])


def row_sums(labels, rows, values):
    place = lax.broadcasted_iota(jnp.int32, (rows, labels.shape[0]), 0)
    selector = (place == labels[None, :]).astype(jnp.bfloat16)
    return jnp.einsum("sn,ntp->tsp", selector, values, preferred_element_type=jnp.float32)


def call(body, operands, shapes, scratch=(), to_hbm=False):
    vmem = pl.BlockSpec(memory_space=pltpu.VMEM)
    out = pl.BlockSpec(memory_space=pl.ANY) if to_hbm else vmem
    moved = sum(a.size for a in operands) + sum(s[0] * s[1] for s in shapes)
    return pl.pallas_call(
        body,
        out_shape=[jax.ShapeDtypeStruct(s, jnp.float32) for s in shapes],
        in_specs=[vmem] * len(operands),
        out_specs=[out] * len(shapes),
        scratch_shapes=list(scratch),
        compiler_params=pltpu.CompilerParams(vmem_limit_bytes=GRANT),
        cost_estimate=pl.CostEstimate(flops=8 * moved, bytes_accessed=4 * moved, transcendentals=0),
    )(*operands)


def prepare_kernel(rates_ref, level_ref, spread_ref, rate_out, level_out, spread_out, coef_out, slab_ref):
    dates_dev, sets, paths = rate_out.shape
    count, mine = lax.axis_size("date"), lax.axis_index("date")
    trade = lax.axis_index("trade")
    lanes = pl.ds(pl.multiple_of(trade * sets, sets), sets)

    def across(row):
        return jnp.broadcast_to(jnp.transpose(jnp.broadcast_to(row, (8, sets)))[:, :1], (sets, paths))

    here = rates_ref[pl.ds(pl.multiple_of(mine * dates_dev, dates_dev), dates_dev), lanes]
    columns = jnp.transpose(here)
    for t in range(dates_dev):
        rate_out[t] = jnp.broadcast_to(columns[:, t : t + 1], (sets, paths))
    level_out[...] = across(level_ref[pl.ds(trade, 1), :])
    spread_out[...] = across(spread_ref[pl.ds(trade, 1), :])
    for d in range(count):
        total = rates_ref[pl.ds(d * dates_dev, 1), lanes]
        for t in range(1, dates_dev):
            total = total * rates_ref[pl.ds(d * dates_dev + t, 1), lanes]
        slab_ref[pl.ds(d, 1), :] = total

    def product(base, length):
        total = slab_ref[pl.ds(base, 1), :]
        for i in range(1, length):
            total = total * slab_ref[pl.ds(base + i, 1), :]
        return total

    before, bit, stage = jnp.ones((1, sets), jnp.float32), 1, 0
    while bit < count:
        base = mine - mine % (2 * bit)
        coef_out[2 * stage] = across(before)
        coef_out[2 * stage + 1] = across(product(base + bit, bit))
        before = jnp.where(mine % (2 * bit) >= bit, before * product(base, bit), before)
        bit, stage = 2 * bit, stage + 1


def net(now, lagged, level):
    return now - (jnp.maximum(lagged - level, 0.0) - jnp.maximum(-lagged - level, 0.0))


def dates_of(refs):
    return [(ref, i) for ref in refs for i in range(ref.shape[0])]


def readers(split, refs, first):
    rim_count, early_dates = split
    own_ref, other_ref = refs[:2]
    late_refs = refs[2 : 2 + rim_count]
    rim_refs = refs[2 + rim_count : 2 + 2 * rim_count]

    def added(t):
        return lambda rows: own_ref[t, rows, :] + other_ref[t, rows, :]

    def plain(ref, i):
        return lambda rows: ref[i, rows, :]

    def masked(ref, i):
        return lambda rows: jnp.where(first, 0.0, ref[i, rows, :])

    sums = [added(t) for t in range(early_dates)] + [plain(*at) for at in dates_of(late_refs)]
    rims = [masked(*at) for at in dates_of(rim_refs)]
    return sums, rims, refs[2 + 2 * rim_count :]


def cost_kernel(split, *refs):
    first = lax.axis_index("date") == 0
    sums, rims, (level_ref, spread_ref, rate_ref, cost_out, last_out) = readers(split, refs, first)
    sets, paths = level_ref.shape
    for start in range(0, sets, BLOCK):
        rows = pl.ds(start, BLOCK)
        level, spread = level_ref[rows, :], spread_ref[rows, :]
        held = []
        state = jnp.zeros((BLOCK, paths), jnp.float32)
        for t in range(len(sums)):
            held.append(sums[t](rows))
            lagged = rims[t](rows) if t < LAG else held[t - LAG]
            cost = spread * jnp.maximum(net(held[t], lagged, level), 0.0)
            cost_out[t, rows, :] = cost
            state = rate_ref[t, rows, :] * state + cost
        last_out[rows, :] = state


def sent_out(out, held_ref, sem, start, dates_dev):
    rows = pl.ds(start * dates_dev, BLOCK * dates_dev)
    return pltpu.make_async_copy(held_ref.at[rows, :], out.at[rows, :], sem.at[start // BLOCK])


def exposure_kernel(split, *refs):
    first = lax.axis_index("date") == 0
    sums, rims, (level_ref, out, held_ref, sem) = readers(split, refs, first)
    sets, _ = level_ref.shape
    dates_dev = len(sums)
    for start in range(0, sets, BLOCK):
        rows = pl.ds(start, BLOCK)
        level = level_ref[rows, :]
        held = []
        for t in range(dates_dev):
            held.append(sums[t](rows))
            lagged = rims[t](rows) if t < LAG else held[t - LAG]
            held_ref[pl.ds(start * dates_dev + t, BLOCK, stride=dates_dev), :] = net(held[t], lagged, level)
        sent_out(out, held_ref, sem, start, dates_dev).start()
    for start in range(0, sets, BLOCK):
        sent_out(out, held_ref, sem, start, dates_dev).wait()


def join_kernel(bit, group_ref, other_ref, rate_ref, out):
    upper = lax.axis_index("date") % (2 * bit) >= bit
    group, other, rate = group_ref[...], other_ref[...], rate_ref[...]
    earlier, later = jnp.where(upper, other, group), jnp.where(upper, group, other)
    out[...] = rate * earlier + later


def funding_kernel(stages, *refs):
    others = refs[:stages]
    coef_ref, cost_ref, rate_ref, out, held_ref, sem = refs[stages:]
    dates_dev, sets, paths = cost_ref.shape
    mine = lax.axis_index("date")
    for start in range(0, sets, BLOCK):
        rows = pl.ds(start, BLOCK)
        state = jnp.zeros((BLOCK, paths), jnp.float32)
        for stage in range(stages):
            upper = mine % (2 << stage) >= (1 << stage)
            longer = state + coef_ref[2 * stage, rows, :] * others[stage][rows, :]
            state = jnp.where(upper, longer, state)
        for t in range(dates_dev):
            state = rate_ref[t, rows, :] * state + cost_ref[t, rows, :]
            held_ref[pl.ds(start * dates_dev + t, BLOCK, stride=dates_dev), :] = state
        sent_out(out, held_ref, sem, start, dates_dev).start()
    for start in range(0, sets, BLOCK):
        sent_out(out, held_ref, sem, start, dates_dev).wait()


def shards(trade_values, set_of_trade, thresholds, spreads, retention):
    set_count = thresholds.shape[0]
    dates_dev, paths = trade_values.shape[1:]
    n_trade = lax.axis_size("trade")
    sets = set_count // n_trade
    offset = set_of_trade - lax.axis_index("trade") * sets
    offset = jnp.where(offset < 0, offset + set_count, offset)
    early_dates = dates_dev - LAG
    bounds = [early_dates]
    for size in RIM_PIECES:
        bounds.append(bounds[-1] + size)
    spans = list(zip(bounds[:-1], bounds[1:]))

    cross = lax.optimization_barrier(row_sums(offset - sets, sets, trade_values))
    late_in = []
    for low, high in spans:
        late_in.append(ahead(cross[low:high], "trade"))
    other = ahead(cross[:early_dates], "trade")
    own = row_sums(offset, sets, trade_values)
    late, rims = [], []
    for k, (low, high) in enumerate(spans):
        mine = own if k == 0 else lax.optimization_barrier((own, late[-1]))[0]
        sums = mine[low:high] + late_in[k]
        rims.append(ahead(sums, "date"))
        late.append(sums)

    count = lax.axis_size("date")
    stages = count.bit_length() - 1
    tall, wide, flat = (dates_dev, sets, paths), (sets, paths), (sets * dates_dev, paths)
    rate_all, level_all, spread_all, coefs = call(
        prepare_kernel,
        (retention.T, thresholds.reshape(n_trade, sets), spreads.reshape(n_trade, sets)),
        (tall, wide, wide, (2 * stages, *wide)),
        [pltpu.VMEM((count, sets), jnp.float32)],
    )

    split = (len(spans), early_dates)
    parts = (own, other, *late, *rims)
    blocks = sets // BLOCK
    leaving = [pltpu.VMEM(flat, jnp.float32), pltpu.SemaphoreType.DMA((blocks,))]
    costs, group = call(functools.partial(cost_kernel, split), (*parts, level_all, spread_all, rate_all), (tall, wide))
    (net_exposure,) = call(functools.partial(exposure_kernel, split), (*parts, level_all), (flat,), leaving, True)
    others = []
    for stage in range(stages):
        others.append(exchanged(group, "date", 1 << stage))
        if stage + 1 < stages:
            (group,) = call(
                functools.partial(join_kernel, 1 << stage), (group, others[-1], coefs[2 * stage + 1]), (wide,)
            )
    (funding,) = call(
        functools.partial(funding_kernel, stages), (*others, coefs, costs, rate_all), (flat,), leaving, True
    )
    shape = (sets, dates_dev, paths)
    return net_exposure.reshape(shape), funding.reshape(shape)


def solution(mesh):
    return jax.shard_map(
        shards,
        mesh=mesh,
        in_specs=(P("trade", "date", "path"), P("trade"), P(), P(), P()),
        out_specs=(P("trade", "date", "path"), P("trade", "date", "path")),
        check_vma=False,
    )
```

time: 108 us -> 50.8 us (0.47); the launches traced: 107 us -> 50.6 us
  blocking collectives: 32.5 us -> 0 us
  local copies, waits for them, and re-layouts: 27.3 us -> 0.99 us
  other arithmetic: 14.9 us -> 0.93 us
  waiting for transfers between devices: 22.4 us -> 31.4 us
  starting transfers between devices: 7.56 us -> 11.8 us
  Pallas kernels: 0 us -> 3.5 us
    all_gather x2 -> x0, blocking collectives: 32.5 us -> none  [entering(): pieces = jax.tree.map(lambda part: lax.all_gather(part, axis), value)]
    pad x12 -> x0, local copies, waits for them, and re-layouts: 13.5 us -> none  [settle(): lax.associative_scan(compose, (rates[:, :, None], costs), axis=1)]
    add x16 -> x3, other arithmetic: 10 us -> 0.09 us  [shards(): sums = mine[low:high] + late_in[k]]
    ppermute x2 -> x9, waiting for transfers between devices: 22.4 us -> 31.4 us  [the longest x7 23.6 us: ahead(): lax.ppermute(value, axis, [(i, (i + 1) % count) for i in range(count)])]
    unnamed x22 -> x8, local copies, waits for them, and re-layouts: 7.51 us -> 0.92 us
    ppermute x2 -> x9, starting transfers between devices: 7.56 us -> 11.8 us  [the longest x7 10.6 us: ahead(): lax.ppermute(value, axis, [(i, (i + 1) % count) for i in range(count)])]
    slice x8 -> x3, local copies, waits for them, and re-layouts: 3.58 us -> 0.07 us  [the longest x2 0.05 us: shards(): late_in.append(ahead(cross[low:high], 'trade'))]
    pallas_call x0 -> x5, Pallas kernels: none -> 3.5 us  [call(): pl.pallas_call(body, out_shape=[jax.ShapeDtypeStruct(s, jnp.float32) for...]
  transfers between devices with their start and end apart: 2 -> 9, of which waited for: 1 -> 7; matrix products, arithmetic and copies ran while one was open for 2% -> 2% of each run, Pallas kernels for 0% -> 4%
where the time goes in v2:
time: 50.8 us; the launch traced here: 50.6 us
  waiting for transfers between devices  31.4 us (62%)
  starting transfers between devices  11.8 us (23%)
  Pallas kernels  3.5 us (7%)
  matrix products  1.25 us (2%)
  local copies, waits for them, and re-layouts  0.99 us (2%)
  other arithmetic  0.93 us (2%)
  between operations  0.72 us (1%)
    ppermute x7, waiting for transfers between devices, ahead(): lax.ppermute(value, axis, [(i, (i + 1) % count) for i in range(count)])  23.6 us
    ppermute x7, starting transfers between devices, ahead(): lax.ppermute(value, axis, [(i, (i + 1) % count) for i in range(count)])  10.6 us
    ppermute x2, waiting for transfers between devices, exchanged(): lax.ppermute(value, axis, [(i, i ^ bit) for i in range(lax.axis_size(axis...  7.8 us
    pallas_call x5, Pallas kernels, call(): pl.pallas_call(body, out_shape=[jax.ShapeDtypeStruct(s, jnp.float32) for...  3.5 us
    dot_general x2, matrix products, row_sums(): jnp.einsum('sn,ntp->tsp', selector, values, preferred_element_type=jnp.fl...  1.25 us
    ppermute x2, starting transfers between devices, exchanged(): lax.ppermute(value, axis, [(i, i ^ bit) for i in range(lax.axis_size(axis...  1.24 us
  transfers between devices with their start and end apart: 9, of which 7 were waited for; matrix products, arithmetic and copies ran while one was open for 2% of the time, Pallas kernels for 4%

profile of v2, /device:TPU:0, one launch (start us, length us, event | category | flops | bytes accessed | tf_op | source)
XLA Modules:
  0.0 50.6 jit_solution(16055248870019603033)
XLA Ops:
  0.6 0.8 %broadcast_add_fusion = (s32[640]{0:T(1024)S(1)}, s32[640]{0:T(1024)S(1)}) fusion(s32[640]{0:T(1024)} %param.6, s32[]{:T(128)S(6)} %mul.3), kind=kLoop, calls=%fused_computation.17 | loop fusion | flops 3200 | bytes 7684 | tf_op jit(solution)/shard_map/sub | solution.py:192
  1.5 0.9 %copy-done = bf16[640,16,128]{2,1,0:T(8,128)(2,1)S(1)} copy-done((bf16[640,16,128]{2,1,0:T(8,128)(2,1)S(1)}, bf16[640,16,128]{2,1,0:T(8,128)(2,1)}, u32[]{:S(2)}) %copy-start) | copy-done | bytes 2621464
  2.4 0.6 %fusion.7 = f32[16,128,128]{2,1,0:T(8,128)S(1)} fusion(bf16[640,16,128]{2,1,0:T(8,128)(2,1)S(1)} %copy-done, s32[640]{0:T(1024)S(1)} %get-tuple-element.18), kind=kOutput, calls=%fused_computation.5 | convolution fusion | flops 335626240 | bytes 3672576 | tf_op jit(solution)/shard_map/sn,ntp->tsp/dot_general | solution.py:29
  3.1 3.1 %collective-permute-start.1 = (f32[3,128,128]{2,1,0:T(8,128)S(1)}, f32[3,128,128]{2,1,0:T(8,128)S(1)}, u32[]{:S(2)}, u32[]{:S(2)}) collective-permute-start(f32[3,128,128]{2,1,0:T(8,128)S(1)} %get-tuple-element.21), channel_id=1, source_target_pairs={{0,16},{16,0},{1,17},{17,1},{2,18},{18,2},{3,19},{19,3},{4,20},{20... | collective-permute-start | bytes 589832 | tf_op jit(solution)/shard_map/ppermute | solution.py:19
  6.1 0.1 collective-permute-start.2
  6.2 2.0 %collective-permute-start.3 = (f32[4,128,128]{2,1,0:T(8,128)S(1)}, f32[4,128,128]{2,1,0:T(8,128)S(1)}, u32[]{:S(2)}, u32[]{:S(2)}) collective-permute-start(f32[4,128,128]{2,1,0:T(8,128)S(1)} %slice.36), channel_id=1, source_target_pairs={{0,16},{16,0},{1,17},{17,1},{2,18},{18,2},{3,19},{19,3},{4,20},{20... | collective-permute-start | bytes 786440 | tf_op jit(solution)/shard_map/ppermute | solution.py:19
  8.3 0.1 collective-permute-start
  8.4 0.6 %fusion.4.refs_0_ = f32[16,128,128]{2,1,0:T(8,128)S(1)} fusion(bf16[640,16,128]{2,1,0:T(8,128)(2,1)S(1)} %copy-done, s32[640]{0:T(1024)S(1)} %get-tuple-element.19), kind=kOutput, calls=%fused_computation.4 | convolution fusion | flops 335626240 | bytes 3672576 | tf_op jit(solution)/shard_map/sn,ntp->tsp/dot_general | solution.py:29
  9.0 2.8 %collective-permute-done.1 = f32[3,128,128]{2,1,0:T(8,128)S(1)} collective-permute-done((f32[3,128,128]{2,1,0:T(8,128)S(1)}, f32[3,128,128]{2,1,0:T(8,128)S(1)}, u32[]{:S(2)}, u32[]{:S(2)}) %collective-permute-start.1) | collective-permute-done | bytes 196640 | tf_op jit(solution)/shard_map/ppermute | solution.py:19
  11.9 4.2 %collective-permute-done.2 = f32[3,128,128]{2,1,0:T(8,128)S(1)} collective-permute-done((f32[3,128,128]{2,1,0:T(8,128)S(1)}, f32[3,128,128]{2,1,0:T(8,128)S(1)}, u32[]{:S(2)}, u32[]{:S(2)}) %collective-permute-start.2) | collective-permute-done | bytes 196640 | tf_op jit(solution)/shard_map/ppermute | solution.py:19
  16.1 5.6 %collective-permute-done.3 = f32[4,128,128]{2,1,0:T(8,128)S(1)} collective-permute-done((f32[4,128,128]{2,1,0:T(8,128)S(1)}, f32[4,128,128]{2,1,0:T(8,128)S(1)}, u32[]{:S(2)}, u32[]{:S(2)}) %collective-permute-start.3) | collective-permute-done | bytes 262176 | tf_op jit(solution)/shard_map/ppermute | solution.py:19
  21.7 2.1 %collective-permute-start.6 = (f32[4,128,128]{2,1,0:T(8,128)S(1)}, f32[4,128,128]{2,1,0:T(8,128)S(1)}, u32[]{:S(2)}, u32[]{:S(2)}) collective-permute-start(f32[4,128,128]{2,1,0:T(8,128)S(1)} %slice_add_fusion.refs_4_), channel_id=1, source_target_pairs={{0,4},{4,8},{8,12},{12,0},{1,5},{5,9},{9,13},{13,1},{2,6},{6,10},{... | collective-permute-start | bytes 786440 | tf_op jit(solution)/shard_map/ppermute | solution.py:19
  23.9 1.6 %collective-permute-start.5 = (f32[3,128,128]{2,1,0:T(8,128)S(1)}, f32[3,128,128]{2,1,0:T(8,128)S(1)}, u32[]{:S(2)}, u32[]{:S(2)}) collective-permute-start(f32[3,128,128]{2,1,0:T(8,128)S(1)} %slice_add_fusion.2.refs_3_), channel_id=1, source_target_pairs={{0,4},{4,8},{8,12},{12,0},{1,5},{5,9},{9,13},{13,1},{2,6},{6,10},{... | collective-permute-start | bytes 589832 | tf_op jit(solution)/shard_map/ppermute | solution.py:19
  25.4 1.6 %collective-permute-start.4 = (f32[3,128,128]{2,1,0:T(8,128)S(1)}, f32[3,128,128]{2,1,0:T(8,128)S(1)}, u32[]{:S(2)}, u32[]{:S(2)}) collective-permute-start(f32[3,128,128]{2,1,0:T(8,128)S(1)} %slice_add_fusion.1.refs_2_), channel_id=1, source_target_pairs={{0,4},{4,8},{8,12},{12,0},{1,5},{5,9},{9,13},{13,1},{2,6},{6,10},{... | collective-permute-start | bytes 589832 | tf_op jit(solution)/shard_map/ppermute | solution.py:19
  27.0 0.6 %shard_map.68 = (f32[16,128,128]{2,1,0:T(8,128)S(1)}, f32[128,128]{1,0:T(8,128)S(1)}, f32[128,128]{1,0:T(8,128)S(1)}, f32[4,128,128]{2,1,0:T(8,128)S(1)}) custom-call(f32[64,256]{1,0:T(8,128)S(1)} %bitcast.17, f32[2,128]{1,0:T(2,128)S(1)} %bitcast.18, f32[2,128]{1,0:T(2,128)S(1)} %bitcast.19), custom_call_target="tpu_custom_call" | custom-call | flops 417792 | bytes 208896 | tf_op jit(solution)/shard_map/pallas_call | solution.py:36
  27.6 8.9 %collective-permute-done.5.refs_6_ = f32[3,128,128]{2,1,0:T(8,128)S(1)} collective-permute-done((f32[3,128,128]{2,1,0:T(8,128)S(1)}, f32[3,128,128]{2,1,0:T(8,128)S(1)}, u32[]{:S(2)}, u32[]{:S(2)}) %collective-permute-start.5) | collective-permute-done | bytes 196640 | tf_op jit(solution)/shard_map/ppermute | solution.py:19
  36.5 2.1 %collective-permute-done.4.refs_5_ = f32[3,128,128]{2,1,0:T(8,128)S(1)} collective-permute-done((f32[3,128,128]{2,1,0:T(8,128)S(1)}, f32[3,128,128]{2,1,0:T(8,128)S(1)}, u32[]{:S(2)}, u32[]{:S(2)}) %collective-permute-start.4) | collective-permute-done | bytes 196640 | tf_op jit(solution)/shard_map/ppermute | solution.py:19
  38.6 0.4 shard_map.70
  39.1 0.1 collective-permute-start.7
  39.2 4.5 %collective-permute-done.7.other_ref.refs_0_ = f32[128,128]{1,0:T(8,128)S(1)} collective-permute-done((f32[128,128]{1,0:T(8,128)S(1)}, f32[128,128]{1,0:T(8,128)S(1)}, u32[]{:S(2)}, u32[]{:S(2)}) %collective-permute-start.7) | collective-permute-done | bytes 65568 | tf_op jit(solution)/shard_map/ppermute | solution.py:23
  43.7 1.2 %collective-permute-start.8 = (f32[128,128]{1,0:T(8,128)S(1)}, f32[128,128]{1,0:T(8,128)S(1)}, u32[]{:S(2)}, u32[]{:S(2)}) collective-permute-start(f32[128,128]{1,0:T(8,128)S(1)} %shard_map.71), channel_id=1, source_target_pairs={{0,8},{4,12},{8,0},{12,4},{1,9},{5,13},{9,1},{13,5},{2,10},{6,14},... | collective-permute-start | bytes 196616 | tf_op jit(solution)/shard_map/ppermute | solution.py:23
  44.9 1.3 %shard_map.69 = f32[2048,128]{1,0:T(8,128)} custom-call(f32[16,128,128]{2,1,0:T(8,128)S(1)} %fusion.4.refs_0_, f32[6,128,128]{2,1,0:T(8,128)S(1)} %collective-permute-done.refs_1_, f32[3,128,128]{2,1,0:T(8,128)S(1)} %slice_add_fusion.1.refs_2_, f32[3,128,128]{2,1,0:T(8,128)S(1)} %slice_add_fusion.2.refs_3_, f32[4,128,128]{2,1,0:T(8,128)S(1)} %slice_add_fusion.refs_4_, ...), custom_call_target="tpu_custom_call" | custom-call | flops 7733248 | bytes 3866624 | tf_op jit(solution)/shard_map/pallas_call | solution.py:36
  46.2 3.3 %collective-permute-done.8.refs_1_ = f32[128,128]{1,0:T(8,128)S(1)} collective-permute-done((f32[128,128]{1,0:T(8,128)S(1)}, f32[128,128]{1,0:T(8,128)S(1)}, u32[]{:S(2)}, u32[]{:S(2)}) %collective-permute-start.8) | collective-permute-done | bytes 65568 | tf_op jit(solution)/shard_map/ppermute | solution.py:23
  49.4 1.2 %shard_map.72 = f32[2048,128]{1,0:T(8,128)} custom-call(f32[128,128]{1,0:T(8,128)S(1)} %collective-permute-done.7.other_ref.refs_0_, f32[128,128]{1,0:T(8,128)S(1)} %collective-permute-done.8.refs_1_, f32[4,128,128]{2,1,0:T(8,128)S(1)} %get-tuple-element.16.refs_2_, f32[16,128,128]{2,1,0:T(8,128)S(1)} %get-tuple-element.17.refs_3_, ...), custom_call_target="tpu_custom_call" | custom-call | flops 7077888 | bytes 3538944 | tf_op jit(solution)/shard_map/pallas_call | solution.py:36
  (17 shorter events, 0.2 us)
Async XLA Ops:
  0.6 1.8 %copy-start = (bf16[640,16,128]{2,1,0:T(8,128)(2,1)S(1)}, bf16[640,16,128]{2,1,0:T(8,128)(2,1)}, u32[]{:S(2)}) copy-start(bf16[640,16,128]{2,1,0:T(8,128)(2,1)} %param.5) | copy-start | bytes 7864324
  3.1 8.8 %collective-permute-start.1 = (f32[3,128,128]{2,1,0:T(8,128)S(1)}, f32[3,128,128]{2,1,0:T(8,128)S(1)}, u32[]{:S(2)}, u32[]{:S(2)}) collective-permute-start(f32[3,128,128]{2,1,0:T(8,128)S(1)} %get-tuple-element.21), channel_id=1, source_target_pairs={{0,16},{16,0},{1,17},{17,1},{2,18},{18,2},{3,19},{19,3},{4,20},{20... | collective-permute-start | bytes 589832 | tf_op jit(solution)/shard_map/ppermute | solution.py:19
  6.1 10.0 %collective-permute-start.2 = (f32[3,128,128]{2,1,0:T(8,128)S(1)}, f32[3,128,128]{2,1,0:T(8,128)S(1)}, u32[]{:S(2)}, u32[]{:S(2)}) collective-permute-start(f32[3,128,128]{2,1,0:T(8,128)S(1)} %get-tuple-element.20), channel_id=1, source_target_pairs={{0,16},{16,0},{1,17},{17,1},{2,18},{18,2},{3,19},{19,3},{4,20},{20... | collective-permute-start | bytes 589832 | tf_op jit(solution)/shard_map/ppermute | solution.py:19
  6.2 15.5 %collective-permute-start.3 = (f32[4,128,128]{2,1,0:T(8,128)S(1)}, f32[4,128,128]{2,1,0:T(8,128)S(1)}, u32[]{:S(2)}, u32[]{:S(2)}) collective-permute-start(f32[4,128,128]{2,1,0:T(8,128)S(1)} %slice.36), channel_id=1, source_target_pairs={{0,16},{16,0},{1,17},{17,1},{2,18},{18,2},{3,19},{19,3},{4,20},{20... | collective-permute-start | bytes 786440 | tf_op jit(solution)/shard_map/ppermute | solution.py:19
  8.3 30.4 %collective-permute-start = (f32[6,128,128]{2,1,0:T(8,128)S(1)}, f32[6,128,128]{2,1,0:T(8,128)S(1)}, u32[]{:S(2)}, u32[]{:S(2)}) collective-permute-start(f32[6,128,128]{2,1,0:T(8,128)S(1)} %slice.32), channel_id=1, source_target_pairs={{0,16},{16,0},{1,17},{17,1},{2,18},{18,2},{3,19},{19,3},{4,20},{20... | collective-permute-start | bytes 1179656 | tf_op jit(solution)/shard_map/ppermute | solution.py:19
  8.4 18.6 %copy-start.1 = (f32[256,64]{0,1:T(8,128)S(1)}, f32[256,64]{0,1:T(8,128)}, u32[]{:S(2)}) copy-start(f32[256,64]{0,1:T(8,128)} %param.9) | copy-start | bytes 196612
  8.4 18.6 %copy-start.2 = (f32[256]{0:T(256)S(1)}, f32[256]{0:T(256)}, u32[]{:S(2)}) copy-start(f32[256]{0:T(256)} %param.7) | copy-start | bytes 3076
  8.4 18.6 %copy-start.3 = (f32[256]{0:T(256)S(1)}, f32[256]{0:T(256)}, u32[]{:S(2)}) copy-start(f32[256]{0:T(256)} %param.8) | copy-start | bytes 3076
  21.7 16.9 %collective-permute-start.6 = (f32[4,128,128]{2,1,0:T(8,128)S(1)}, f32[4,128,128]{2,1,0:T(8,128)S(1)}, u32[]{:S(2)}, u32[]{:S(2)}) collective-permute-start(f32[4,128,128]{2,1,0:T(8,128)S(1)} %slice_add_fusion.refs_4_), channel_id=1, source_target_pairs={{0,4},{4,8},{8,12},{12,0},{1,5},{5,9},{9,13},{13,1},{2,6},{6,10},{... | collective-permute-start | bytes 786440 | tf_op jit(solution)/shard_map/ppermute | solution.py:19
  23.9 12.7 %collective-permute-start.5 = (f32[3,128,128]{2,1,0:T(8,128)S(1)}, f32[3,128,128]{2,1,0:T(8,128)S(1)}, u32[]{:S(2)}, u32[]{:S(2)}) collective-permute-start(f32[3,128,128]{2,1,0:T(8,128)S(1)} %slice_add_fusion.2.refs_3_), channel_id=1, source_target_pairs={{0,4},{4,8},{8,12},{12,0},{1,5},{5,9},{9,13},{13,1},{2,6},{6,10},{... | collective-permute-start | bytes 589832 | tf_op jit(solution)/shard_map/ppermute | solution.py:19
  25.4 13.2 %collective-permute-start.4 = (f32[3,128,128]{2,1,0:T(8,128)S(1)}, f32[3,128,128]{2,1,0:T(8,128)S(1)}, u32[]{:S(2)}, u32[]{:S(2)}) collective-permute-start(f32[3,128,128]{2,1,0:T(8,128)S(1)} %slice_add_fusion.1.refs_2_), channel_id=1, source_target_pairs={{0,4},{4,8},{8,12},{12,0},{1,5},{5,9},{9,13},{13,1},{2,6},{6,10},{... | collective-permute-start | bytes 589832 | tf_op jit(solution)/shard_map/ppermute | solution.py:19
  39.1 4.6 %collective-permute-start.7 = (f32[128,128]{1,0:T(8,128)S(1)}, f32[128,128]{1,0:T(8,128)S(1)}, u32[]{:S(2)}, u32[]{:S(2)}) collective-permute-start(f32[128,128]{1,0:T(8,128)S(1)} %get-tuple-element.15.group_ref), channel_id=1, source_target_pairs={{0,4},{4,0},{8,12},{12,8},{1,5},{5,1},{9,13},{13,9},{2,6},{6,2},{1... | collective-permute-start | bytes 196616 | tf_op jit(solution)/shard_map/ppermute | solution.py:23
  43.7 5.7 %collective-permute-start.8 = (f32[128,128]{1,0:T(8,128)S(1)}, f32[128,128]{1,0:T(8,128)S(1)}, u32[]{:S(2)}, u32[]{:S(2)}) collective-permute-start(f32[128,128]{1,0:T(8,128)S(1)} %shard_map.71), channel_id=1, source_target_pairs={{0,8},{4,12},{8,0},{12,4},{1,9},{5,13},{9,1},{13,5},{2,10},{6,14},... | collective-permute-start | bytes 196616 | tf_op jit(solution)/shard_map/ppermute | solution.py:23

commit v3 on v0

v3 whole, which is shorter than its diff:
```python
import functools

import jax
import jax.numpy as jnp
from jax import lax
from jax.experimental import pallas as pl
from jax.experimental.pallas import tpu as pltpu
from jax.sharding import PartitionSpec as P


LAG = 10
GRANT = 8 * 1024 * 1024
LAST_PART = 2
BLOCK = 32


def ahead(value, axis):
    count = lax.axis_size(axis)
    return lax.ppermute(value, axis, [(i, (i + 1) % count) for i in range(count)])


def exchanged(value, axis, bit):
    return lax.ppermute(value, axis, [(i, i ^ bit) for i in range(lax.axis_size(axis))])


def row_sums(labels, rows, values):
    place = lax.broadcasted_iota(jnp.int32, (rows, labels.shape[0]), 0)
    selector = (place == labels[None, :]).astype(jnp.bfloat16)
    return jnp.einsum("sn,ntp->tsp", selector, values, preferred_element_type=jnp.float32)


def group_bounds(sets):
    cut = sets - sets // LAST_PART
    return [(0, cut), (cut, sets)]


def call(body, operands, shapes, scratch=(), to_hbm=False, into=None):
    vmem, hbm = pl.BlockSpec(memory_space=pltpu.VMEM), pl.BlockSpec(memory_space=pl.ANY)
    out = hbm if to_hbm else vmem
    kept = () if into is None else (into,)
    moved = sum(a.size for a in operands) + sum(s[0] * s[1] for s in shapes)
    return pl.pallas_call(
        body,
        out_shape=[jax.ShapeDtypeStruct(s, jnp.float32) for s in shapes],
        in_specs=[vmem] * len(operands) + [hbm] * len(kept),
        out_specs=[out] * len(shapes),
        scratch_shapes=list(scratch),
        compiler_params=pltpu.CompilerParams(vmem_limit_bytes=GRANT),
        cost_estimate=pl.CostEstimate(flops=8 * moved, bytes_accessed=4 * moved, transcendentals=0),
        input_output_aliases={len(operands): 0} if kept else {},
    )(*operands, *kept)


def prepare_kernel(rates_ref, level_ref, spread_ref, rate_out, level_out, spread_out, coef_out, slab_ref):
    dates_dev, sets, paths = rate_out.shape
    count, mine = lax.axis_size("date"), lax.axis_index("date")
    trade = lax.axis_index("trade")
    lanes = pl.ds(pl.multiple_of(trade * sets, sets), sets)

    def across(row):
        return jnp.broadcast_to(jnp.transpose(jnp.broadcast_to(row, (8, sets)))[:, :1], (sets, paths))

    here = rates_ref[pl.ds(pl.multiple_of(mine * dates_dev, dates_dev), dates_dev), lanes]
    columns = jnp.transpose(here)
    for t in range(dates_dev):
        rate_out[t] = jnp.broadcast_to(columns[:, t : t + 1], (sets, paths))
    level_out[...] = across(level_ref[pl.ds(trade, 1), :])
    spread_out[...] = across(spread_ref[pl.ds(trade, 1), :])
    for d in range(count):
        total = rates_ref[pl.ds(d * dates_dev, 1), lanes]
        for t in range(1, dates_dev):
            total = total * rates_ref[pl.ds(d * dates_dev + t, 1), lanes]
        slab_ref[pl.ds(d, 1), :] = total

    bit, stage = count // 2, 0
    while bit:
        base = mine - mine % (2 * bit)
        lower = beyond = jnp.ones((1, sets), jnp.float32)
        for i in range(bit):
            rate = slab_ref[pl.ds(base + i, 1), :]
            lower = lower * rate
            beyond = beyond * jnp.where(base + i > mine, rate, 1.0)
        coef_out[2 * stage] = across(lower)
        coef_out[2 * stage + 1] = across(beyond)
        bit, stage = bit // 2, stage + 1


def net(now, lagged, level):
    return now - (jnp.maximum(lagged - level, 0.0) - jnp.maximum(-lagged - level, 0.0))


def exposures(begin, pieces, refs, use):
    own_ref, other_ref = refs[:2]
    late_refs, rim_refs = refs[2 : 2 + pieces], refs[2 + pieces : 2 + 2 * pieces]
    level_ref = refs[2 + 2 * pieces]
    first = lax.axis_index("date") == 0
    early = other_ref.shape[0]
    dates_dev = own_ref.shape[0]
    for piece in range(pieces):
        inside = pl.ds(piece * BLOCK, BLOCK)
        rows = pl.ds(begin + piece * BLOCK, BLOCK)
        level = level_ref[rows, :]
        held, found = [], []
        for t in range(dates_dev):
            if t < early:
                held.append(own_ref[t, rows, :] + other_ref[t, inside, :])
            else:
                held.append(late_refs[piece][t - early])
            lagged = held[t - LAG] if t >= LAG else jnp.where(first, 0.0, rim_refs[piece][t])
            found.append(net(held[t], lagged, level))
        use(piece, inside, rows, found)


def cost_kernel(begin, pieces, *refs):
    spread_ref, rate_ref, coef_ref, cost_out, last_out, sent_out_ref = refs[3 + 2 * pieces :]

    def use(piece, inside, rows, found):
        spread = spread_ref[rows, :]
        state = jnp.zeros_like(spread)
        for t, exposure in enumerate(found):
            cost = spread * jnp.maximum(exposure, 0.0)
            cost_out[t, inside, :] = cost
            state = rate_ref[t, rows, :] * state + cost
        last_out[inside, :] = state
        sent_out_ref[inside, :] = state * coef_ref[1, rows, :]

    exposures(begin, pieces, refs, use)


def sent_out(out, held_ref, sem, begin, piece, dates_dev):
    rows = pl.ds(piece * BLOCK * dates_dev, BLOCK * dates_dev)
    there = pl.ds((begin + piece * BLOCK) * dates_dev, BLOCK * dates_dev)
    return pltpu.make_async_copy(held_ref.at[rows, :], out.at[there, :], sem.at[piece])


def exposure_kernel(begin, pieces, *refs):
    out, held_ref, sem = refs[-3:]
    dates_dev = refs[0].shape[0]

    def use(piece, inside, rows, found):
        for t, exposure in enumerate(found):
            held_ref[pl.ds(piece * BLOCK * dates_dev + t, BLOCK, stride=dates_dev), :] = exposure
        sent_out(out, held_ref, sem, begin, piece, dates_dev).start()

    exposures(begin, pieces, refs, use)
    for piece in range(pieces):
        sent_out(out, held_ref, sem, begin, piece, dates_dev).wait()


def entering(stages, others, coef_ref, inside, rows):
    mine, count = lax.axis_index("date"), lax.axis_size("date")
    arrived = jnp.where(mine >= count // 2, others[0][inside, :], 0.0)
    for stage in range(1, stages):
        upper = mine & (count >> (stage + 1)) != 0
        kept = jnp.where(upper, arrived * coef_ref[2 * stage, rows, :], arrived)
        arrived = kept + others[stage][inside, :]
    return arrived


def join_kernel(begin, stage, last_ref, coef_ref, *refs):
    inside, rows = pl.ds(0, last_ref.shape[0]), pl.ds(begin, last_ref.shape[0])
    arrived = entering(stage, refs[:-1], coef_ref, inside, rows)
    longer = arrived * coef_ref[2 * stage, rows, :] + last_ref[...] * coef_ref[2 * stage + 1, rows, :]
    upper = lax.axis_index("date") & (lax.axis_size("date") >> (stage + 1)) != 0
    refs[-1][...] = jnp.where(upper, arrived, longer)


def funding_kernel(begin, pieces, stages, *refs):
    coef_ref, cost_ref, rate_ref = refs[stages : stages + 3]
    out, held_ref, sem = refs[-3:]
    dates_dev = rate_ref.shape[0]
    for piece in range(pieces):
        inside = pl.ds(piece * BLOCK, BLOCK)
        rows = pl.ds(begin + piece * BLOCK, BLOCK)
        state = entering(stages, refs[:stages], coef_ref, inside, rows)
        for t in range(dates_dev):
            state = rate_ref[t, rows, :] * state + cost_ref[t, inside, :]
            held_ref[pl.ds(piece * BLOCK * dates_dev + t, BLOCK, stride=dates_dev), :] = state
        sent_out(out, held_ref, sem, begin, piece, dates_dev).start()
    for piece in range(pieces):
        sent_out(out, held_ref, sem, begin, piece, dates_dev).wait()


def shards(trade_values, set_of_trade, thresholds, spreads, retention):
    set_count = thresholds.shape[0]
    dates_dev, paths = trade_values.shape[1:]
    n_trade = lax.axis_size("trade")
    sets = set_count // n_trade
    offset = set_of_trade - lax.axis_index("trade") * sets
    offset = jnp.where(offset < 0, offset + set_count, offset)
    early = dates_dev - LAG
    pieces = [slice(low, low + BLOCK) for low in range(0, sets, BLOCK)]
    groups = group_bounds(sets)

    cross = lax.optimization_barrier(row_sums(offset - sets, sets, trade_values))
    late_in, other = [], []
    for rows in pieces:
        late_in.append(ahead(cross[early:, rows], "trade"))
    for low, high in groups:
        other.append(ahead(cross[:early, low:high], "trade"))
    own = row_sums(offset, sets, trade_values)
    late, rims = [], []
    for k, rows in enumerate(pieces):
        mine = own if k == 0 else lax.optimization_barrier((own, late[-1]))[0]
        sums = mine[early:, rows] + late_in[k]
        rims.append(ahead(sums, "date"))
        late.append(sums)

    count = lax.axis_size("date")
    stages = count.bit_length() - 1
    tall, wide = (dates_dev, sets, paths), (sets, paths)
    rate_all, level_all, spread_all, coefs = call(
        prepare_kernel,
        (retention.T, thresholds.reshape(n_trade, sets), spreads.reshape(n_trade, sets)),
        (tall, wide, wide, (2 * stages, *wide)),
        [pltpu.VMEM((count, sets), jnp.float32)],
    )

    flat = (sets * dates_dev, paths)
    net_exposure = funding = None
    for g, (low, high) in enumerate(groups):
        size = high - low
        mine = range(low // BLOCK, high // BLOCK)
        parts = (own, other[g], *[late[k] for k in mine], *[rims[k] for k in mine], level_all)
        leaving = [pltpu.VMEM((size * dates_dev, paths), jnp.float32), pltpu.SemaphoreType.DMA((len(mine),))]
        costs, last, sent = call(
            functools.partial(cost_kernel, low, len(mine)),
            (*parts, spread_all, rate_all, coefs),
            ((dates_dev, size, paths), (size, paths), (size, paths)),
        )
        net_exposure = call(
            functools.partial(exposure_kernel, low, len(mine)), parts, (flat,), leaving, True, net_exposure
        )[0]
        others = []
        for stage in range(stages):
            if stage:
                (sent,) = call(functools.partial(join_kernel, low, stage), (last, coefs, *others), ((size, paths),))
            others.append(exchanged(sent, "date", count >> (stage + 1)))
        funding = call(
            functools.partial(funding_kernel, low, len(mine), stages),
            (*others, coefs, costs, rate_all),
            (flat,),
            leaving,
            True,
            funding,
        )[0]
    shape = (sets, dates_dev, paths)
    return net_exposure.reshape(shape), funding.reshape(shape)


def solution(mesh):
    return jax.shard_map(
        shards,
        mesh=mesh,
        in_specs=(P("trade", "date", "path"), P("trade"), P(), P(), P()),
        out_specs=(P("trade", "date", "path"), P("trade", "date", "path")),
        check_vma=False,
    )
```

time: 108 us -> 51 us (0.47)
  blocking collectives: 32.5 us -> 0 us
  local copies, waits for them, and re-layouts: 27.3 us -> 0.99 us
  other arithmetic: 14.9 us -> 0.95 us
  starting transfers between devices: 7.56 us -> 17.1 us
  Pallas kernels: 0 us -> 5.06 us
  waiting for transfers between devices: 22.4 us -> 24.7 us
    all_gather x2 -> x0, blocking collectives: 32.5 us -> none  [entering(): pieces = jax.tree.map(lambda part: lax.all_gather(part, axis), value)]
    pad x12 -> x0, local copies, waits for them, and re-layouts: 13.5 us -> none  [settle(): lax.associative_scan(compose, (rates[:, :, None], costs), axis=1)]
    add x16 -> x4, other arithmetic: 10 us -> 0.1 us  [shards(): sums = mine[early:, rows] + late_in[k]]
    ppermute x2 -> x14, starting transfers between devices: 7.56 us -> 17.1 us  [the longest x10 14.3 us: ahead(): lax.ppermute(value, axis, [(i, (i + 1) % count) for i in range(count)])]
    unnamed x22 -> x8, local copies, waits for them, and re-layouts: 7.51 us -> 0.92 us
    pallas_call x0 -> x9, Pallas kernels: none -> 5.06 us  [call(): pl.pallas_call(body, out_shape=[jax.ShapeDtypeStruct(s, jnp.float32) for...]
    slice x8 -> x2, local copies, waits for them, and re-layouts: 3.58 us -> 0.07 us  [the longest x1 0.05 us: shards(): late_in.append(ahead(cross[early:, rows], 'trade'))]
    ppermute x2 -> x14, waiting for transfers between devices: 22.4 us -> 24.7 us  [the longest x10 20.9 us: ahead(): lax.ppermute(value, axis, [(i, (i + 1) % count) for i in range(count)])]
  transfers between devices with their start and end apart: 2 -> 14, of which waited for: 1 -> 7; matrix products, arithmetic and copies ran while one was open for 2% -> 1% of each run, Pallas kernels for 0% -> 8%
where the time goes in v3:
time: 51 us; the launch traced here: 50.8 us
  waiting for transfers between devices  24.7 us (48%)
  starting transfers between devices  17.1 us (34%)
  Pallas kernels  5.06 us (10%)
  matrix products  1.25 us (2%)
  local copies, waits for them, and re-layouts  0.99 us (2%)
  other arithmetic  0.95 us (2%)
  between operations  0.77 us (2%)
    ppermute x10, waiting for transfers between devices, ahead(): lax.ppermute(value, axis, [(i, (i + 1) % count) for i in range(count)])  20.9 us
    ppermute x10, starting transfers between devices, ahead(): lax.ppermute(value, axis, [(i, (i + 1) % count) for i in range(count)])  14.3 us
    pallas_call x9, Pallas kernels, call(): pl.pallas_call(body, out_shape=[jax.ShapeDtypeStruct(s, jnp.float32) for...  5.06 us
    ppermute x4, waiting for transfers between devices, exchanged(): lax.ppermute(value, axis, [(i, i ^ bit) for i in range(lax.axis_size(axis...  3.76 us
    ppermute x4, starting transfers between devices, exchanged(): lax.ppermute(value, axis, [(i, i ^ bit) for i in range(lax.axis_size(axis...  2.82 us
    dot_general x2, matrix products, row_sums(): jnp.einsum('sn,ntp->tsp', selector, values, preferred_element_type=jnp.fl...  1.25 us
  transfers between devices with their start and end apart: 14, of which 7 were waited for; matrix products, arithmetic and copies ran while one was open for 1% of the time, Pallas kernels for 8%

profile of v3, /device:TPU:0, one launch (start us, length us, event | category | flops | bytes accessed | tf_op | source)
XLA Modules:
  0.0 50.8 jit_solution(5517338836737536145)
XLA Ops:
  0.6 0.8 %broadcast_add_fusion = (s32[640]{0:T(1024)S(1)}, s32[640]{0:T(1024)S(1)}) fusion(s32[640]{0:T(1024)} %param.6, s32[]{:T(128)S(6)} %mul.3), kind=kLoop, calls=%fused_computation.17 | loop fusion | flops 3200 | bytes 7684 | tf_op jit(solution)/shard_map/sub | solution.py:195
  1.5 0.9 %copy-done = bf16[640,16,128]{2,1,0:T(8,128)(2,1)S(1)} copy-done((bf16[640,16,128]{2,1,0:T(8,128)(2,1)S(1)}, bf16[640,16,128]{2,1,0:T(8,128)(2,1)}, u32[]{:S(2)}) %copy-start) | copy-done | bytes 2621464
  3.1 3.1 %collective-permute-start.4 = (f32[10,32,128]{2,1,0:T(8,128)S(1)}, f32[10,32,128]{2,1,0:T(8,128)S(1)}, u32[]{:S(2)}, u32[]{:S(2)}) collective-permute-start(f32[10,32,128]{2,1,0:T(8,128)S(1)} %get-tuple-element.32), channel_id=1, source_target_pairs={{0,16},{16,0},{1,17},{17,1},{2,18},{18,2},{3,19},{19,3},{4,20},{20... | collective-permute-start | bytes 491528 | tf_op jit(solution)/shard_map/ppermute | solution.py:19
  6.2 1.9 %collective-permute-start.2 = (f32[10,32,128]{2,1,0:T(8,128)S(1)}, f32[10,32,128]{2,1,0:T(8,128)S(1)}, u32[]{:S(2)}, u32[]{:S(2)}) collective-permute-start(f32[10,32,128]{2,1,0:T(8,128)S(1)} %get-tuple-element.34), channel_id=1, source_target_pairs={{0,16},{16,0},{1,17},{17,1},{2,18},{18,2},{3,19},{19,3},{4,20},{20... | collective-permute-start | bytes 491528 | tf_op jit(solution)/shard_map/ppermute | solution.py:19
  8.3 2.0 %collective-permute-start.7 = (f32[6,64,128]{2,1,0:T(8,128)S(1)}, f32[6,64,128]{2,1,0:T(8,128)S(1)}, u32[]{:S(2)}, u32[]{:S(2)}) collective-permute-start(f32[6,64,128]{2,1,0:T(8,128)S(1)} %get-tuple-element.30), channel_id=1, source_target_pairs={{0,16},{16,0},{1,17},{17,1},{2,18},{18,2},{3,19},{19,3},{4,20},{20... | collective-permute-start | bytes 589832 | tf_op jit(solution)/shard_map/ppermute | solution.py:19
  10.3 0.6 %fusion.4.refs_0_ = f32[16,128,128]{2,1,0:T(8,128)S(1)} fusion(bf16[640,16,128]{2,1,0:T(8,128)(2,1)S(1)} %copy-done, s32[640]{0:T(1024)S(1)} %get-tuple-element.29), kind=kOutput, calls=%fused_computation.4 | convolution fusion | flops 335626240 | bytes 3672576 | tf_op jit(solution)/shard_map/sn,ntp->tsp/dot_general | solution.py:29
  10.9 10.8 %collective-permute-done.1 = f32[10,32,128]{2,1,0:T(8,128)S(1)} collective-permute-done((f32[10,32,128]{2,1,0:T(8,128)S(1)}, f32[10,32,128]{2,1,0:T(8,128)S(1)}, u32[]{:S(2)}, u32[]{:S(2)}) %collective-permute-start.1) | collective-permute-done | bytes 163872 | tf_op jit(solution)/shard_map/ppermute | solution.py:19
  21.7 2.0 %collective-permute-start = (f32[6,64,128]{2,1,0:T(8,128)S(1)}, f32[6,64,128]{2,1,0:T(8,128)S(1)}, u32[]{:S(2)}, u32[]{:S(2)}) collective-permute-start(f32[6,64,128]{2,1,0:T(8,128)S(1)} %get-tuple-element.31), channel_id=1, source_target_pairs={{0,16},{16,0},{1,17},{17,1},{2,18},{18,2},{3,19},{19,3},{4,20},{20... | collective-permute-start | bytes 589832 | tf_op jit(solution)/shard_map/ppermute | solution.py:19
  23.8 1.6 %collective-permute-start.9 = (f32[10,32,128]{2,1,0:T(8,128)S(1)}, f32[10,32,128]{2,1,0:T(8,128)S(1)}, u32[]{:S(2)}, u32[]{:S(2)}) collective-permute-start(f32[10,32,128]{2,1,0:T(8,128)S(1)} %slice_add_fusion.3.refs_3_), channel_id=1, source_target_pairs={{0,4},{4,8},{8,12},{12,0},{1,5},{5,9},{9,13},{13,1},{2,6},{6,10},{... | collective-permute-start | bytes 491528 | tf_op jit(solution)/shard_map/ppermute | solution.py:19
  25.4 1.6 %collective-permute-start.8 = (f32[10,32,128]{2,1,0:T(8,128)S(1)}, f32[10,32,128]{2,1,0:T(8,128)S(1)}, u32[]{:S(2)}, u32[]{:S(2)}) collective-permute-start(f32[10,32,128]{2,1,0:T(8,128)S(1)} %slice_add_fusion.refs_2_), channel_id=1, source_target_pairs={{0,4},{4,8},{8,12},{12,0},{1,5},{5,9},{9,13},{13,1},{2,6},{6,10},{... | collective-permute-start | bytes 491528 | tf_op jit(solution)/shard_map/ppermute | solution.py:19
  27.1 1.6 %collective-permute-start.6 = (f32[10,32,128]{2,1,0:T(8,128)S(1)}, f32[10,32,128]{2,1,0:T(8,128)S(1)}, u32[]{:S(2)}, u32[]{:S(2)}) collective-permute-start(f32[10,32,128]{2,1,0:T(8,128)S(1)} %slice_add_fusion.1.refs_3_), channel_id=1, source_target_pairs={{0,4},{4,8},{8,12},{12,0},{1,5},{5,9},{9,13},{13,1},{2,6},{6,10},{... | collective-permute-start | bytes 491528 | tf_op jit(solution)/shard_map/ppermute | solution.py:19
  29.0 0.7 %shard_map.68 = (f32[16,128,128]{2,1,0:T(8,128)S(1)}, f32[128,128]{1,0:T(8,128)S(1)}, f32[128,128]{1,0:T(8,128)S(1)}, f32[4,128,128]{2,1,0:T(8,128)S(1)}) custom-call(f32[64,256]{1,0:T(8,128)S(1)} %bitcast.15, f32[2,128]{1,0:T(2,128)S(1)} %bitcast.16, f32[2,128]{1,0:T(2,128)S(1)} %bitcast.17), custom_call_target="tpu_custom_call" | custom-call | flops 417792 | bytes 208896 | tf_op jit(solution)/shard_map/pallas_call | solution.py:42
  29.6 3.1 %collective-permute-done.9.refs_5_ = f32[10,32,128]{2,1,0:T(8,128)S(1)} collective-permute-done((f32[10,32,128]{2,1,0:T(8,128)S(1)}, f32[10,32,128]{2,1,0:T(8,128)S(1)}, u32[]{:S(2)}, u32[]{:S(2)}) %collective-permute-start.9) | collective-permute-done | bytes 163872 | tf_op jit(solution)/shard_map/ppermute | solution.py:19
  32.7 3.6 %collective-permute-done.8.refs_4_ = f32[10,32,128]{2,1,0:T(8,128)S(1)} collective-permute-done((f32[10,32,128]{2,1,0:T(8,128)S(1)}, f32[10,32,128]{2,1,0:T(8,128)S(1)}, u32[]{:S(2)}, u32[]{:S(2)}) %collective-permute-start.8) | collective-permute-done | bytes 163872 | tf_op jit(solution)/shard_map/ppermute | solution.py:19
  36.6 0.8 %collective-permute-start.12 = (f32[64,128]{1,0:T(8,128)S(1)}, f32[64,128]{1,0:T(8,128)S(1)}, u32[]{:S(2)}, u32[]{:S(2)}) collective-permute-start(f32[64,128]{1,0:T(8,128)S(1)} %get-tuple-element.25), channel_id=1, source_target_pairs={{0,8},{4,12},{8,0},{12,4},{1,9},{5,13},{9,1},{13,5},{2,10},{6,14},... | collective-permute-start | bytes 98312 | tf_op jit(solution)/shard_map/ppermute | solution.py:23
  37.3 1.3 %collective-permute-done.6.refs_5_ = f32[10,32,128]{2,1,0:T(8,128)S(1)} collective-permute-done((f32[10,32,128]{2,1,0:T(8,128)S(1)}, f32[10,32,128]{2,1,0:T(8,128)S(1)}, u32[]{:S(2)}, u32[]{:S(2)}) %collective-permute-start.6) | collective-permute-done | bytes 163872 | tf_op jit(solution)/shard_map/ppermute | solution.py:19
  38.6 2.1 %collective-permute-done.5.refs_4_ = f32[10,32,128]{2,1,0:T(8,128)S(1)} collective-permute-done((f32[10,32,128]{2,1,0:T(8,128)S(1)}, f32[10,32,128]{2,1,0:T(8,128)S(1)}, u32[]{:S(2)}, u32[]{:S(2)}) %collective-permute-start.5) | collective-permute-done | bytes 163872 | tf_op jit(solution)/shard_map/ppermute | solution.py:19
  40.9 1.5 %collective-permute-start.10 = (f32[64,128]{1,0:T(8,128)S(1)}, f32[64,128]{1,0:T(8,128)S(1)}, u32[]{:S(2)}, u32[]{:S(2)}) collective-permute-start(f32[64,128]{1,0:T(8,128)S(1)} %get-tuple-element.22), channel_id=1, source_target_pairs={{0,8},{4,12},{8,0},{12,4},{1,9},{5,13},{9,1},{13,5},{2,10},{6,14},... | collective-permute-start | bytes 98312 | tf_op jit(solution)/shard_map/ppermute | solution.py:23
  43.0 2.9 %collective-permute-done.10.refs_0_ = f32[64,128]{1,0:T(8,128)S(1)} collective-permute-done((f32[64,128]{1,0:T(8,128)S(1)}, f32[64,128]{1,0:T(8,128)S(1)}, u32[]{:S(2)}, u32[]{:S(2)}) %collective-permute-start.10) | collective-permute-done | bytes 32800 | tf_op jit(solution)/shard_map/ppermute | solution.py:23
  45.9 1.0 %shard_map.69.refs_7_ = f32[2048,128]{1,0:T(8,128)} custom-call(f32[16,128,128]{2,1,0:T(8,128)S(1)} %fusion.4.refs_0_, f32[6,64,128]{2,1,0:T(8,128)S(1)} %collective-permute-done.7.refs_1_, f32[10,32,128]{2,1,0:T(8,128)S(1)} %slice_add_fusion.refs_2_, f32[10,32,128]{2,1,0:T(8,128)S(1)} %slice_add_fusion.3.refs_3_, ...), custom_call_target="tpu_custom_call" | custom-call | flops 6029312 | bytes 3014656 | tf_op jit(solution)/shard_map/pallas_call | solution.py:42
  46.9 1.0 %shard_map.70 = f32[2048,128]{1,0:T(8,128)} custom-call(f32[16,128,128]{2,1,0:T(8,128)S(1)} %fusion.4.refs_0_, f32[6,64,128]{2,1,0:T(8,128)S(1)} %collective-permute-done.refs_1_, f32[10,32,128]{2,1,0:T(8,128)S(1)} %slice_add_fusion.2.refs_2_, f32[10,32,128]{2,1,0:T(8,128)S(1)} %slice_add_fusion.1.refs_3_, ...), custom_call_target="tpu_custom_call", output_to_operand_aliasing={{}: (7, {})} | custom-call | flops 6029312 | bytes 3014656 | tf_op jit(solution)/shard_map/pallas_call | solution.py:42
  47.9 1.0 %shard_map.75.refs_5_ = f32[2048,128]{1,0:T(8,128)} custom-call(f32[64,128]{1,0:T(8,128)S(1)} %collective-permute-done.12.refs_0_, f32[64,128]{1,0:T(8,128)S(1)} %collective-permute-done.13.refs_1_, f32[4,128,128]{2,1,0:T(8,128)S(1)} %get-tuple-element.21.refs_9_.coef_ref.refs_2_, f32[16,64,128]{2,1,0:T(8,128)S(1)} %get-tuple-element.27.refs_3_, ...), custom_call_target="tpu_custom_call" | custom-call | flops 5898240 | bytes 2949120 | tf_op jit(solution)/shard_map/pallas_call | solution.py:42
  48.9 0.9 %collective-permute-done.11.refs_1_ = f32[64,128]{1,0:T(8,128)S(1)} collective-permute-done((f32[64,128]{1,0:T(8,128)S(1)}, f32[64,128]{1,0:T(8,128)S(1)}, u32[]{:S(2)}, u32[]{:S(2)}) %collective-permute-start.11) | collective-permute-done | bytes 32800 | tf_op jit(solution)/shard_map/ppermute | solution.py:23
  49.8 1.0 %shard_map.76 = f32[2048,128]{1,0:T(8,128)} custom-call(f32[64,128]{1,0:T(8,128)S(1)} %collective-permute-done.10.refs_0_, f32[64,128]{1,0:T(8,128)S(1)} %collective-permute-done.11.refs_1_, f32[4,128,128]{2,1,0:T(8,128)S(1)} %get-tuple-element.21.refs_9_.coef_ref.refs_2_, ...), custom_call_target="tpu_custom_call", output_to_operand_aliasing={{}: (5, {})} | custom-call | flops 5898240 | bytes 2949120 | tf_op jit(solution)/shard_map/pallas_call | solution.py:42
  (30 shorter events, 2.2 us)
Async XLA Ops:
  0.6 1.8 %copy-start = (bf16[640,16,128]{2,1,0:T(8,128)(2,1)S(1)}, bf16[640,16,128]{2,1,0:T(8,128)(2,1)}, u32[]{:S(2)}) copy-start(bf16[640,16,128]{2,1,0:T(8,128)(2,1)} %param.5) | copy-start | bytes 7864324
  3.1 24.0 %collective-permute-start.4 = (f32[10,32,128]{2,1,0:T(8,128)S(1)}, f32[10,32,128]{2,1,0:T(8,128)S(1)}, u32[]{:S(2)}, u32[]{:S(2)}) collective-permute-start(f32[10,32,128]{2,1,0:T(8,128)S(1)} %get-tuple-element.32), channel_id=1, source_target_pairs={{0,16},{16,0},{1,17},{17,1},{2,18},{18,2},{3,19},{19,3},{4,20},{20... | collective-permute-start | bytes 491528 | tf_op jit(solution)/shard_map/ppermute | solution.py:19
  6.1 19.3 %collective-permute-start.3 = (f32[10,32,128]{2,1,0:T(8,128)S(1)}, f32[10,32,128]{2,1,0:T(8,128)S(1)}, u32[]{:S(2)}, u32[]{:S(2)}) collective-permute-start(f32[10,32,128]{2,1,0:T(8,128)S(1)} %get-tuple-element.33), channel_id=1, source_target_pairs={{0,16},{16,0},{1,17},{17,1},{2,18},{18,2},{3,19},{19,3},{4,20},{20... | collective-permute-start | bytes 491528 | tf_op jit(solution)/shard_map/ppermute | solution.py:19
  6.2 17.6 %collective-permute-start.2 = (f32[10,32,128]{2,1,0:T(8,128)S(1)}, f32[10,32,128]{2,1,0:T(8,128)S(1)}, u32[]{:S(2)}, u32[]{:S(2)}) collective-permute-start(f32[10,32,128]{2,1,0:T(8,128)S(1)} %get-tuple-element.34), channel_id=1, source_target_pairs={{0,16},{16,0},{1,17},{17,1},{2,18},{18,2},{3,19},{19,3},{4,20},{20... | collective-permute-start | bytes 491528 | tf_op jit(solution)/shard_map/ppermute | solution.py:19
  8.2 13.6 %collective-permute-start.1 = (f32[10,32,128]{2,1,0:T(8,128)S(1)}, f32[10,32,128]{2,1,0:T(8,128)S(1)}, u32[]{:S(2)}, u32[]{:S(2)}) collective-permute-start(f32[10,32,128]{2,1,0:T(8,128)S(1)} %get-tuple-element.35), channel_id=1, source_target_pairs={{0,16},{16,0},{1,17},{17,1},{2,18},{18,2},{3,19},{19,3},{4,20},{20... | collective-permute-start | bytes 491528 | tf_op jit(solution)/shard_map/ppermute | solution.py:19
  8.3 20.4 %collective-permute-start.7 = (f32[6,64,128]{2,1,0:T(8,128)S(1)}, f32[6,64,128]{2,1,0:T(8,128)S(1)}, u32[]{:S(2)}, u32[]{:S(2)}) collective-permute-start(f32[6,64,128]{2,1,0:T(8,128)S(1)} %get-tuple-element.30), channel_id=1, source_target_pairs={{0,16},{16,0},{1,17},{17,1},{2,18},{18,2},{3,19},{19,3},{4,20},{20... | collective-permute-start | bytes 589832 | tf_op jit(solution)/shard_map/ppermute | solution.py:19
  10.3 18.7 %copy-start.1 = (f32[256,64]{0,1:T(8,128)S(1)}, f32[256,64]{0,1:T(8,128)}, u32[]{:S(2)}) copy-start(f32[256,64]{0,1:T(8,128)} %param.9) | copy-start | bytes 196612
  10.3 18.7 %copy-start.2 = (f32[256]{0:T(256)S(1)}, f32[256]{0:T(256)}, u32[]{:S(2)}) copy-start(f32[256]{0:T(256)} %param.7) | copy-start | bytes 3076
  10.3 18.7 %copy-start.3 = (f32[256]{0:T(256)S(1)}, f32[256]{0:T(256)}, u32[]{:S(2)}) copy-start(f32[256]{0:T(256)} %param.8) | copy-start | bytes 3076
  21.7 15.6 %collective-permute-start = (f32[6,64,128]{2,1,0:T(8,128)S(1)}, f32[6,64,128]{2,1,0:T(8,128)S(1)}, u32[]{:S(2)}, u32[]{:S(2)}) collective-permute-start(f32[6,64,128]{2,1,0:T(8,128)S(1)} %get-tuple-element.31), channel_id=1, source_target_pairs={{0,16},{16,0},{1,17},{17,1},{2,18},{18,2},{3,19},{19,3},{4,20},{20... | collective-permute-start | bytes 589832 | tf_op jit(solution)/shard_map/ppermute | solution.py:19
  23.8 8.9 %collective-permute-start.9 = (f32[10,32,128]{2,1,0:T(8,128)S(1)}, f32[10,32,128]{2,1,0:T(8,128)S(1)}, u32[]{:S(2)}, u32[]{:S(2)}) collective-permute-start(f32[10,32,128]{2,1,0:T(8,128)S(1)} %slice_add_fusion.3.refs_3_), channel_id=1, source_target_pairs={{0,4},{4,8},{8,12},{12,0},{1,5},{5,9},{9,13},{13,1},{2,6},{6,10},{... | collective-permute-start | bytes 491528 | tf_op jit(solution)/shard_map/ppermute | solution.py:19
  25.4 10.9 %collective-permute-start.8 = (f32[10,32,128]{2,1,0:T(8,128)S(1)}, f32[10,32,128]{2,1,0:T(8,128)S(1)}, u32[]{:S(2)}, u32[]{:S(2)}) collective-permute-start(f32[10,32,128]{2,1,0:T(8,128)S(1)} %slice_add_fusion.refs_2_), channel_id=1, source_target_pairs={{0,4},{4,8},{8,12},{12,0},{1,5},{5,9},{9,13},{13,1},{2,6},{6,10},{... | collective-permute-start | bytes 491528 | tf_op jit(solution)/shard_map/ppermute | solution.py:19
  27.1 11.5 %collective-permute-start.6 = (f32[10,32,128]{2,1,0:T(8,128)S(1)}, f32[10,32,128]{2,1,0:T(8,128)S(1)}, u32[]{:S(2)}, u32[]{:S(2)}) collective-permute-start(f32[10,32,128]{2,1,0:T(8,128)S(1)} %slice_add_fusion.1.refs_3_), channel_id=1, source_target_pairs={{0,4},{4,8},{8,12},{12,0},{1,5},{5,9},{9,13},{13,1},{2,6},{6,10},{... | collective-permute-start | bytes 491528 | tf_op jit(solution)/shard_map/ppermute | solution.py:19
  28.7 12.0 %collective-permute-start.5 = (f32[10,32,128]{2,1,0:T(8,128)S(1)}, f32[10,32,128]{2,1,0:T(8,128)S(1)}, u32[]{:S(2)}, u32[]{:S(2)}) collective-permute-start(f32[10,32,128]{2,1,0:T(8,128)S(1)} %slice_add_fusion.2.refs_2_), channel_id=1, source_target_pairs={{0,4},{4,8},{8,12},{12,0},{1,5},{5,9},{9,13},{13,1},{2,6},{6,10},{... | collective-permute-start | bytes 491528 | tf_op jit(solution)/shard_map/ppermute | solution.py:19
  36.6 5.9 %collective-permute-start.12 = (f32[64,128]{1,0:T(8,128)S(1)}, f32[64,128]{1,0:T(8,128)S(1)}, u32[]{:S(2)}, u32[]{:S(2)}) collective-permute-start(f32[64,128]{1,0:T(8,128)S(1)} %get-tuple-element.25), channel_id=1, source_target_pairs={{0,8},{4,12},{8,0},{12,4},{1,9},{5,13},{9,1},{13,5},{2,10},{6,14},... | collective-permute-start | bytes 98312 | tf_op jit(solution)/shard_map/ppermute | solution.py:23
  40.9 4.9 %collective-permute-start.10 = (f32[64,128]{1,0:T(8,128)S(1)}, f32[64,128]{1,0:T(8,128)S(1)}, u32[]{:S(2)}, u32[]{:S(2)}) collective-permute-start(f32[64,128]{1,0:T(8,128)S(1)} %get-tuple-element.22), channel_id=1, source_target_pairs={{0,8},{4,12},{8,0},{12,4},{1,9},{5,13},{9,1},{13,5},{2,10},{6,14},... | collective-permute-start | bytes 98312 | tf_op jit(solution)/shard_map/ppermute | solution.py:23
  42.5 5.5 %collective-permute-start.13 = (f32[64,128]{1,0:T(8,128)S(1)}, f32[64,128]{1,0:T(8,128)S(1)}, u32[]{:S(2)}, u32[]{:S(2)}) collective-permute-start(f32[64,128]{1,0:T(8,128)S(1)} %shard_map.74), channel_id=1, source_target_pairs={{0,4},{4,0},{8,12},{12,8},{1,5},{5,1},{9,13},{13,9},{2,6},{6,2},{1... | collective-permute-start | bytes 98312 | tf_op jit(solution)/shard_map/ppermute | solution.py:23
  45.8 4.0 %collective-permute-start.11 = (f32[64,128]{1,0:T(8,128)S(1)}, f32[64,128]{1,0:T(8,128)S(1)}, u32[]{:S(2)}, u32[]{:S(2)}) collective-permute-start(f32[64,128]{1,0:T(8,128)S(1)} %shard_map.72), channel_id=1, source_target_pairs={{0,4},{4,0},{8,12},{12,8},{1,5},{5,1},{9,13},{13,9},{2,6},{6,2},{1... | collective-permute-start | bytes 98312 | tf_op jit(solution)/shard_map/ppermute | solution.py:23

commit v4 on v3

v4 whole, which is shorter than its diff:
```python
import functools
import math

import jax
import jax.numpy as jnp
from jax import lax
from jax.experimental import pallas as pl
from jax.experimental.pallas import tpu as pltpu
from jax.sharding import PartitionSpec as P


LAG = 10
GRANT = 8 * 1024 * 1024
PARTS = ((2, 2), (2, 2))
ROWS = 32
LEAVING = 8


def ahead(value, axis):
    count = lax.axis_size(axis)
    return lax.ppermute(value, axis, [(i, (i + 1) % count) for i in range(count)])


def exchanged(value, axis, bit):
    return lax.ppermute(value, axis, [(i, i ^ bit) for i in range(lax.axis_size(axis))])


def row_sums(labels, rows, values):
    place = lax.broadcasted_iota(jnp.int32, (rows, labels.shape[0]), 0)
    selector = (place == labels[None, :]).astype(jnp.bfloat16)
    return jnp.einsum("sn,ntp->tsp", selector, values, preferred_element_type=jnp.float32)


def parts_of(sets):
    whole = sum(sum(part) for part in PARTS)
    sizes = [[sets * share // whole for share in part] for part in PARTS]
    assert sum(map(sum, sizes)) == sets
    return sizes


def call(body, operands, shapes, scratch=(), to_hbm=False, into=()):
    vmem, hbm = pl.BlockSpec(memory_space=pltpu.VMEM), pl.BlockSpec(memory_space=pl.ANY)
    moved = sum(a.size for a in operands) + sum(s[0] * s[1] for s in shapes)
    return pl.pallas_call(
        body,
        out_shape=[jax.ShapeDtypeStruct(s, jnp.float32) for s in shapes],
        in_specs=[vmem] * len(operands) + [hbm] * len(into),
        out_specs=[hbm if to_hbm else vmem] * len(shapes),
        scratch_shapes=list(scratch),
        compiler_params=pltpu.CompilerParams(vmem_limit_bytes=GRANT),
        cost_estimate=pl.CostEstimate(flops=8 * moved, bytes_accessed=4 * moved, transcendentals=0),
        input_output_aliases={len(operands) + i: i for i in range(len(into))},
    )(*operands, *into)


def prepare_kernel(rates_ref, level_ref, spread_ref, rate_out, level_out, spread_out, coef_out, slab_ref):
    dates_dev, sets, paths = rate_out.shape
    count, mine = lax.axis_size("date"), lax.axis_index("date")
    trade = lax.axis_index("trade")
    lanes = pl.ds(pl.multiple_of(trade * sets, sets), sets)

    def across(row):
        return jnp.broadcast_to(jnp.transpose(jnp.broadcast_to(row, (8, sets)))[:, :1], (sets, paths))

    here = rates_ref[pl.ds(pl.multiple_of(mine * dates_dev, dates_dev), dates_dev), lanes]
    columns = jnp.transpose(here)
    for t in range(dates_dev):
        rate_out[t] = jnp.broadcast_to(columns[:, t : t + 1], (sets, paths))
    level_out[...] = across(level_ref[pl.ds(trade, 1), :])
    spread_out[...] = across(spread_ref[pl.ds(trade, 1), :])
    for d in range(count):
        total = rates_ref[pl.ds(d * dates_dev, 1), lanes]
        for t in range(1, dates_dev):
            total = total * rates_ref[pl.ds(d * dates_dev + t, 1), lanes]
        slab_ref[pl.ds(d, 1), :] = total

    bit, stage = count // 2, 0
    while bit:
        base = mine - mine % (2 * bit)
        lower = beyond = jnp.ones((1, sets), jnp.float32)
        for i in range(bit):
            rate = slab_ref[pl.ds(base + i, 1), :]
            lower = lower * rate
            beyond = beyond * jnp.where(base + i > mine, rate, 1.0)
        coef_out[2 * stage] = across(lower)
        coef_out[2 * stage + 1] = across(beyond)
        bit, stage = bit // 2, stage + 1


def net(now, lagged, level):
    return now - (jnp.maximum(lagged - level, 0.0) - jnp.maximum(-lagged - level, 0.0))


def each_block(begin, pieces, refs, use):
    own_ref, other_ref = refs[:2]
    late_refs, rim_refs = refs[2 : 2 + pieces], refs[2 + pieces : 2 + 2 * pieces]
    level_ref = refs[2 + 2 * pieces]
    first = lax.axis_index("date") == 0
    early, dates_dev = other_ref.shape[0], own_ref.shape[0]
    at = 0
    for late_ref, rim_ref in zip(late_refs, rim_refs):
        size = math.gcd(ROWS, late_ref.shape[1])
        for row in range(0, late_ref.shape[1], size):
            within, inside, rows = pl.ds(row, size), pl.ds(at, size), pl.ds(begin + at, size)
            level = level_ref[rows, :]
            held, found = [], []
            for t in range(dates_dev):
                if t < early:
                    held.append(own_ref[t, rows, :] + other_ref[t, inside, :])
                else:
                    held.append(late_ref[t - early, within, :])
                lagged = held[t - LAG] if t >= LAG else jnp.where(first, 0.0, rim_ref[t, within, :])
                found.append(net(held[t], lagged, level))
            use(at, size, rows, found)
            at += size


def cost_kernel(begin, pieces, *refs):
    spread_ref, rate_ref, coef_ref, cost_out, last_out, sent_out = refs[3 + 2 * pieces :]

    def use(at, size, rows, found):
        inside = pl.ds(at, size)
        spread = spread_ref[rows, :]
        state = jnp.zeros_like(spread)
        for t, exposure in enumerate(found):
            cost = spread * jnp.maximum(exposure, 0.0)
            cost_out[t, inside, :] = cost
            state = rate_ref[t, rows, :] * state + cost
        last_out[inside, :] = state
        sent_out[inside, :] = state * coef_ref[1, rows, :]

    each_block(begin, pieces, refs, use)


def exposure_kernel(begin, pieces, *refs):
    dates_dev = refs[0].shape[0]

    def use(at, size, rows, found):
        for t, exposure in enumerate(found):
            refs[-1][pl.ds(at * dates_dev + t, size, stride=dates_dev), :] = exposure

    each_block(begin, pieces, refs, use)


def entering(stages, others, coef_ref, inside, rows):
    mine, count = lax.axis_index("date"), lax.axis_size("date")
    arrived = jnp.where(mine >= count // 2, others[0][inside, :], 0.0)
    for stage in range(1, stages):
        upper = mine & (count >> (stage + 1)) != 0
        kept = jnp.where(upper, arrived * coef_ref[2 * stage, rows, :], arrived)
        arrived = kept + others[stage][inside, :]
    return arrived


def join_kernel(begin, stage, last_ref, coef_ref, *refs):
    inside, rows = pl.ds(0, last_ref.shape[0]), pl.ds(begin, last_ref.shape[0])
    arrived = entering(stage, refs[:-1], coef_ref, inside, rows)
    longer = arrived * coef_ref[2 * stage, rows, :] + last_ref[...] * coef_ref[2 * stage + 1, rows, :]
    upper = lax.axis_index("date") & (lax.axis_size("date") >> (stage + 1)) != 0
    refs[-1][...] = jnp.where(upper, arrived, longer)


def funding_kernel(begin, stages, *refs):
    coef_ref, cost_ref, rate_ref, net_ref = refs[stages : stages + 4]
    net_out, out, held_ref, sem = refs[-4:]
    dates_dev, size = cost_ref.shape[:2]
    block = LEAVING * dates_dev

    def leaving(part):
        here, there = pl.ds(part * block, block), pl.ds(begin * dates_dev + part * block, block)
        return pltpu.make_async_copy(held_ref.at[here, :], out.at[there, :], sem.at[part + 1])

    there = pl.ds(begin * dates_dev, size * dates_dev)
    exposed = pltpu.make_async_copy(net_ref, net_out.at[there, :], sem.at[0])
    exposed.start()
    parts = range(size // LEAVING)
    for part in parts:
        inside = pl.ds(part * LEAVING, LEAVING)
        rows = pl.ds(begin + part * LEAVING, LEAVING)
        state = entering(stages, refs[:stages], coef_ref, inside, rows)
        for t in range(dates_dev):
            state = rate_ref[t, rows, :] * state + cost_ref[t, inside, :]
            held_ref[pl.ds(part * block + t, LEAVING, stride=dates_dev), :] = state
        leaving(part).start()
    exposed.wait()
    for part in parts:
        leaving(part).wait()


def shards(trade_values, set_of_trade, thresholds, spreads, retention):
    set_count = thresholds.shape[0]
    dates_dev, paths = trade_values.shape[1:]
    n_trade = lax.axis_size("trade")
    sets = set_count // n_trade
    offset = set_of_trade - lax.axis_index("trade") * sets
    offset = jnp.where(offset < 0, offset + set_count, offset)
    early = dates_dev - LAG
    sizes = parts_of(sets)
    pieces, groups, low = [], [], 0
    for part in sizes:
        groups.append((low, low + sum(part), range(len(pieces), len(pieces) + len(part))))
        for size in part:
            pieces.append(slice(low, low + size))
            low += size

    cross = lax.optimization_barrier(row_sums(offset - sets, sets, trade_values))
    late_in, other = [], []
    for rows in pieces:
        late_in.append(ahead(cross[early:, rows], "trade"))
    for low, high, _ in groups:
        other.append(ahead(cross[:early, low:high], "trade"))
    own = row_sums(offset, sets, trade_values)
    late, rims = [], []
    for k, rows in enumerate(pieces):
        mine = own if k == 0 else lax.optimization_barrier((own, late[-1]))[0]
        sums = mine[early:, rows] + late_in[k]
        rims.append(ahead(sums, "date"))
        late.append(sums)

    count = lax.axis_size("date")
    stages = count.bit_length() - 1
    tall, wide = (dates_dev, sets, paths), (sets, paths)
    rate_all, level_all, spread_all, coefs = call(
        prepare_kernel,
        (retention.T, thresholds.reshape(n_trade, sets), spreads.reshape(n_trade, sets)),
        (tall, wide, wide, (2 * stages, *wide)),
        [pltpu.VMEM((count, sets), jnp.float32)],
    )

    flat = (sets * dates_dev, paths)
    results = ()
    for g, (low, high, mine) in enumerate(groups):
        size = high - low
        parts = (own, other[g], *[late[k] for k in mine], *[rims[k] for k in mine])
        costs, last, sent = call(
            functools.partial(cost_kernel, low, len(mine)),
            (*parts, level_all, spread_all, rate_all, coefs),
            ((dates_dev, size, paths), (size, paths), (size, paths)),
        )
        (exposed,) = call(
            functools.partial(exposure_kernel, low, len(mine)), (*parts, level_all), ((size * dates_dev, paths),)
        )
        others = []
        for stage in range(stages):
            if stage:
                (sent,) = call(functools.partial(join_kernel, low, stage), (last, coefs, *others), ((size, paths),))
            others.append(exchanged(sent, "date", count >> (stage + 1)))
        results = call(
            functools.partial(funding_kernel, low, stages),
            (*others, coefs, costs, rate_all, exposed),
            (flat, flat),
            [pltpu.VMEM((size * dates_dev, paths), jnp.float32), pltpu.SemaphoreType.DMA((1 + size // LEAVING,))],
            True,
            results,
        )
    return tuple(result.reshape(sets, dates_dev, paths) for result in results)


def solution(mesh):
    return jax.shard_map(
        shards,
        mesh=mesh,
        in_specs=(P("trade", "date", "path"), P("trade"), P(), P(), P()),
        out_specs=(P("trade", "date", "path"), P("trade", "date", "path")),
        check_vma=False,
    )
```

time: 51 us -> 51 us (level)
  waiting for transfers between devices: 24.7 us -> 26.1 us
  Pallas kernels: 5.06 us -> 3.72 us
    ppermute x4, waiting for transfers between devices: 3.76 us -> 5.16 us  [exchanged(): lax.ppermute(value, axis, [(i, i ^ bit) for i in range(lax.axis_size(axis...]
    pallas_call x9, Pallas kernels: 5.06 us -> 3.72 us  [call(): pl.pallas_call(body, out_shape=[jax.ShapeDtypeStruct(s, jnp.float32) for...]
  transfers between devices with their start and end apart: 14 -> 14, of which waited for: 7 -> 7; matrix products, arithmetic and copies ran while one was open for 1% -> 1% of each run, Pallas kernels for 8% -> 5%
where the time goes in v4:
time: 51 us; the launch traced here: 50.9 us
  waiting for transfers between devices  26.1 us (51%)
  starting transfers between devices  17.1 us (34%)
  Pallas kernels  3.72 us (7%)
  matrix products  1.25 us (2%)
  local copies, waits for them, and re-layouts  0.99 us (2%)
  other arithmetic  0.95 us (2%)
  between operations  0.77 us (2%)
    ppermute x10, waiting for transfers between devices, ahead(): lax.ppermute(value, axis, [(i, (i + 1) % count) for i in range(count)])  20.9 us
    ppermute x10, starting transfers between devices, ahead(): lax.ppermute(value, axis, [(i, (i + 1) % count) for i in range(count)])  14.3 us
    ppermute x4, waiting for transfers between devices, exchanged(): lax.ppermute(value, axis, [(i, i ^ bit) for i in range(lax.axis_size(axis...  5.16 us
    pallas_call x9, Pallas kernels, call(): pl.pallas_call(body, out_shape=[jax.ShapeDtypeStruct(s, jnp.float32) for...  3.72 us
    ppermute x4, starting transfers between devices, exchanged(): lax.ppermute(value, axis, [(i, i ^ bit) for i in range(lax.axis_size(axis...  2.82 us
    dot_general x2, matrix products, row_sums(): jnp.einsum('sn,ntp->tsp', selector, values, preferred_element_type=jnp.fl...  1.25 us
  transfers between devices with their start and end apart: 14, of which 7 were waited for; matrix products, arithmetic and copies ran while one was open for 1% of the time, Pallas kernels for 5%

profile of v4, /device:TPU:0, one launch (start us, length us, event | category | flops | bytes accessed | tf_op | source)
XLA Modules:
  0.0 50.9 jit_solution(4546380018099701199)
XLA Ops:
  0.6 0.8 %broadcast_add_fusion = (s32[640]{0:T(1024)S(1)}, s32[640]{0:T(1024)S(1)}) fusion(s32[640]{0:T(1024)} %param.6, s32[]{:T(128)S(6)} %mul.3), kind=kLoop, calls=%fused_computation.17 | loop fusion | flops 3200 | bytes 7684 | tf_op jit(solution)/shard_map/sub | solution.py:206
  1.5 0.9 %copy-done = bf16[640,16,128]{2,1,0:T(8,128)(2,1)S(1)} copy-done((bf16[640,16,128]{2,1,0:T(8,128)(2,1)S(1)}, bf16[640,16,128]{2,1,0:T(8,128)(2,1)}, u32[]{:S(2)}) %copy-start) | copy-done | bytes 2621464
  2.4 0.6 %fusion.7 = f32[16,128,128]{2,1,0:T(8,128)S(1)} fusion(bf16[640,16,128]{2,1,0:T(8,128)(2,1)S(1)} %copy-done, s32[640]{0:T(1024)S(1)} %get-tuple-element.36), kind=kOutput, calls=%fused_computation.5 | convolution fusion | flops 335626240 | bytes 3672576 | tf_op jit(solution)/shard_map/sn,ntp->tsp/dot_general | solution.py:31
  3.1 3.1 %collective-permute-start.4 = (f32[10,32,128]{2,1,0:T(8,128)S(1)}, f32[10,32,128]{2,1,0:T(8,128)S(1)}, u32[]{:S(2)}, u32[]{:S(2)}) collective-permute-start(f32[10,32,128]{2,1,0:T(8,128)S(1)} %get-tuple-element.40), channel_id=1, source_target_pairs={{0,16},{16,0},{1,17},{17,1},{2,18},{18,2},{3,19},{19,3},{4,20},{20... | collective-permute-start | bytes 491528 | tf_op jit(solution)/shard_map/ppermute | solution.py:21
  6.2 1.9 %collective-permute-start.2 = (f32[10,32,128]{2,1,0:T(8,128)S(1)}, f32[10,32,128]{2,1,0:T(8,128)S(1)}, u32[]{:S(2)}, u32[]{:S(2)}) collective-permute-start(f32[10,32,128]{2,1,0:T(8,128)S(1)} %get-tuple-element.42), channel_id=1, source_target_pairs={{0,16},{16,0},{1,17},{17,1},{2,18},{18,2},{3,19},{19,3},{4,20},{20... | collective-permute-start | bytes 491528 | tf_op jit(solution)/shard_map/ppermute | solution.py:21
  8.3 2.0 %collective-permute-start.9 = (f32[6,64,128]{2,1,0:T(8,128)S(1)}, f32[6,64,128]{2,1,0:T(8,128)S(1)}, u32[]{:S(2)}, u32[]{:S(2)}) collective-permute-start(f32[6,64,128]{2,1,0:T(8,128)S(1)} %get-tuple-element.38), channel_id=1, source_target_pairs={{0,16},{16,0},{1,17},{17,1},{2,18},{18,2},{3,19},{19,3},{4,20},{20... | collective-permute-start | bytes 589832 | tf_op jit(solution)/shard_map/ppermute | solution.py:21
  10.3 0.6 %fusion.4.refs_0_ = f32[16,128,128]{2,1,0:T(8,128)S(1)} fusion(bf16[640,16,128]{2,1,0:T(8,128)(2,1)S(1)} %copy-done, s32[640]{0:T(1024)S(1)} %get-tuple-element.37), kind=kOutput, calls=%fused_computation.4 | convolution fusion | flops 335626240 | bytes 3672576 | tf_op jit(solution)/shard_map/sn,ntp->tsp/dot_general | solution.py:31
  10.9 10.8 %collective-permute-done.1 = f32[10,32,128]{2,1,0:T(8,128)S(1)} collective-permute-done((f32[10,32,128]{2,1,0:T(8,128)S(1)}, f32[10,32,128]{2,1,0:T(8,128)S(1)}, u32[]{:S(2)}, u32[]{:S(2)}) %collective-permute-start.1) | collective-permute-done | bytes 163872 | tf_op jit(solution)/shard_map/ppermute | solution.py:21
  21.7 2.0 %collective-permute-start = (f32[6,64,128]{2,1,0:T(8,128)S(1)}, f32[6,64,128]{2,1,0:T(8,128)S(1)}, u32[]{:S(2)}, u32[]{:S(2)}) collective-permute-start(f32[6,64,128]{2,1,0:T(8,128)S(1)} %get-tuple-element.39), channel_id=1, source_target_pairs={{0,16},{16,0},{1,17},{17,1},{2,18},{18,2},{3,19},{19,3},{4,20},{20... | collective-permute-start | bytes 589832 | tf_op jit(solution)/shard_map/ppermute | solution.py:21
  23.8 1.6 %collective-permute-start.11 = (f32[10,32,128]{2,1,0:T(8,128)S(1)}, f32[10,32,128]{2,1,0:T(8,128)S(1)}, u32[]{:S(2)}, u32[]{:S(2)}) collective-permute-start(f32[10,32,128]{2,1,0:T(8,128)S(1)} %slice_add_fusion.3.refs_3_), channel_id=1, source_target_pairs={{0,4},{4,8},{8,12},{12,0},{1,5},{5,9},{9,13},{13,1},{2,6},{6,10},{... | collective-permute-start | bytes 491528 | tf_op jit(solution)/shard_map/ppermute | solution.py:21
  25.4 1.6 %collective-permute-start.10 = (f32[10,32,128]{2,1,0:T(8,128)S(1)}, f32[10,32,128]{2,1,0:T(8,128)S(1)}, u32[]{:S(2)}, u32[]{:S(2)}) collective-permute-start(f32[10,32,128]{2,1,0:T(8,128)S(1)} %slice_add_fusion.refs_2_), channel_id=1, source_target_pairs={{0,4},{4,8},{8,12},{12,0},{1,5},{5,9},{9,13},{13,1},{2,6},{6,10},{... | collective-permute-start | bytes 491528 | tf_op jit(solution)/shard_map/ppermute | solution.py:21
  27.1 1.6 %collective-permute-start.6 = (f32[10,32,128]{2,1,0:T(8,128)S(1)}, f32[10,32,128]{2,1,0:T(8,128)S(1)}, u32[]{:S(2)}, u32[]{:S(2)}) collective-permute-start(f32[10,32,128]{2,1,0:T(8,128)S(1)} %slice_add_fusion.1.refs_3_), channel_id=1, source_target_pairs={{0,4},{4,8},{8,12},{12,0},{1,5},{5,9},{9,13},{13,1},{2,6},{6,10},{... | collective-permute-start | bytes 491528 | tf_op jit(solution)/shard_map/ppermute | solution.py:21
  29.0 0.7 %shard_map.68 = (f32[16,128,128]{2,1,0:T(8,128)S(1)}, f32[128,128]{1,0:T(8,128)S(1)}, f32[128,128]{1,0:T(8,128)S(1)}, f32[4,128,128]{2,1,0:T(8,128)S(1)}) custom-call(f32[64,256]{1,0:T(8,128)S(1)} %bitcast.15, f32[2,128]{1,0:T(2,128)S(1)} %bitcast.16, f32[2,128]{1,0:T(2,128)S(1)} %bitcast.17), custom_call_target="tpu_custom_call" | custom-call | flops 417792 | bytes 208896 | tf_op jit(solution)/shard_map/pallas_call | solution.py:44
  29.6 3.1 %collective-permute-done.11.refs_5_ = f32[10,32,128]{2,1,0:T(8,128)S(1)} collective-permute-done((f32[10,32,128]{2,1,0:T(8,128)S(1)}, f32[10,32,128]{2,1,0:T(8,128)S(1)}, u32[]{:S(2)}, u32[]{:S(2)}) %collective-permute-start.11) | collective-permute-done | bytes 163872 | tf_op jit(solution)/shard_map/ppermute | solution.py:21
  32.7 3.6 %collective-permute-done.10.refs_4_ = f32[10,32,128]{2,1,0:T(8,128)S(1)} collective-permute-done((f32[10,32,128]{2,1,0:T(8,128)S(1)}, f32[10,32,128]{2,1,0:T(8,128)S(1)}, u32[]{:S(2)}, u32[]{:S(2)}) %collective-permute-start.10) | collective-permute-done | bytes 163872 | tf_op jit(solution)/shard_map/ppermute | solution.py:21
  36.6 0.8 %collective-permute-start.12 = (f32[64,128]{1,0:T(8,128)S(1)}, f32[64,128]{1,0:T(8,128)S(1)}, u32[]{:S(2)}, u32[]{:S(2)}) collective-permute-start(f32[64,128]{1,0:T(8,128)S(1)} %get-tuple-element.29), channel_id=1, source_target_pairs={{0,8},{4,12},{8,0},{12,4},{1,9},{5,13},{9,1},{13,5},{2,10},{6,14},... | collective-permute-start | bytes 98312 | tf_op jit(solution)/shard_map/ppermute | solution.py:25
  37.3 1.3 %collective-permute-done.6.refs_5_ = f32[10,32,128]{2,1,0:T(8,128)S(1)} collective-permute-done((f32[10,32,128]{2,1,0:T(8,128)S(1)}, f32[10,32,128]{2,1,0:T(8,128)S(1)}, u32[]{:S(2)}, u32[]{:S(2)}) %collective-permute-start.6) | collective-permute-done | bytes 163872 | tf_op jit(solution)/shard_map/ppermute | solution.py:21
  38.6 2.1 %collective-permute-done.5.refs_4_ = f32[10,32,128]{2,1,0:T(8,128)S(1)} collective-permute-done((f32[10,32,128]{2,1,0:T(8,128)S(1)}, f32[10,32,128]{2,1,0:T(8,128)S(1)}, u32[]{:S(2)}, u32[]{:S(2)}) %collective-permute-start.5) | collective-permute-done | bytes 163872 | tf_op jit(solution)/shard_map/ppermute | solution.py:21
  40.9 1.5 %collective-permute-start.7 = (f32[64,128]{1,0:T(8,128)S(1)}, f32[64,128]{1,0:T(8,128)S(1)}, u32[]{:S(2)}, u32[]{:S(2)}) collective-permute-start(f32[64,128]{1,0:T(8,128)S(1)} %get-tuple-element.26), channel_id=1, source_target_pairs={{0,8},{4,12},{8,0},{12,4},{1,9},{5,13},{9,1},{13,5},{2,10},{6,14},... | collective-permute-start | bytes 98312 | tf_op jit(solution)/shard_map/ppermute | solution.py:25
  42.5 0.5 collective-permute-start.13
  43.0 2.9 %collective-permute-done.7.refs_0_ = f32[64,128]{1,0:T(8,128)S(1)} collective-permute-done((f32[64,128]{1,0:T(8,128)S(1)}, f32[64,128]{1,0:T(8,128)S(1)}, u32[]{:S(2)}, u32[]{:S(2)}) %collective-permute-start.7) | collective-permute-done | bytes 32800 | tf_op jit(solution)/shard_map/ppermute | solution.py:25
  46.5 1.0 %shard_map.75 = (f32[2048,128]{1,0:T(8,128)}, f32[2048,128]{1,0:T(8,128)}) custom-call(f32[64,128]{1,0:T(8,128)S(1)} %collective-permute-done.12.refs_0_, f32[64,128]{1,0:T(8,128)S(1)} %collective-permute-done.13.refs_1_, f32[4,128,128]{2,1,0:T(8,128)S(1)} %get-tuple-element.25.refs_9_.coef_ref.refs_2_, f32[16,64,128]{2,1,0:T(8,128)S(1)} %get-tuple-element.31.refs_3_, ...), custom_call_target="tpu_custom_call" | custom-call | flops 9043968 | bytes 4521984 | tf_op jit(solution)/shard_map/pallas_call | solution.py:44
  47.5 2.3 %collective-permute-done.8.refs_1_ = f32[64,128]{1,0:T(8,128)S(1)} collective-permute-done((f32[64,128]{1,0:T(8,128)S(1)}, f32[64,128]{1,0:T(8,128)S(1)}, u32[]{:S(2)}, u32[]{:S(2)}) %collective-permute-start.8) | collective-permute-done | bytes 32800 | tf_op jit(solution)/shard_map/ppermute | solution.py:25
  49.8 1.0 %shard_map.76 = (f32[2048,128]{1,0:T(8,128)}, f32[2048,128]{1,0:T(8,128)}) custom-call(f32[64,128]{1,0:T(8,128)S(1)} %collective-permute-done.7.refs_0_, f32[64,128]{1,0:T(8,128)S(1)} %collective-permute-done.8.refs_1_, f32[4,128,128]{2,1,0:T(8,128)S(1)} %get-tuple-element.25.refs_9_.coef_ref.refs_2_, ...), custom_call_target="tpu_custom_call", output_to_operand_aliasing={{0}: (6, {}), {1}: (7, {})} | custom-call | flops 9043968 | bytes 4521984 | tf_op jit(solution)/shard_map/pallas_call | solution.py:44
  (30 shorter events, 1.7 us)
Async XLA Ops:
  0.6 1.8 %copy-start = (bf16[640,16,128]{2,1,0:T(8,128)(2,1)S(1)}, bf16[640,16,128]{2,1,0:T(8,128)(2,1)}, u32[]{:S(2)}) copy-start(bf16[640,16,128]{2,1,0:T(8,128)(2,1)} %param.5) | copy-start | bytes 7864324
  3.1 24.0 %collective-permute-start.4 = (f32[10,32,128]{2,1,0:T(8,128)S(1)}, f32[10,32,128]{2,1,0:T(8,128)S(1)}, u32[]{:S(2)}, u32[]{:S(2)}) collective-permute-start(f32[10,32,128]{2,1,0:T(8,128)S(1)} %get-tuple-element.40), channel_id=1, source_target_pairs={{0,16},{16,0},{1,17},{17,1},{2,18},{18,2},{3,19},{19,3},{4,20},{20... | collective-permute-start | bytes 491528 | tf_op jit(solution)/shard_map/ppermute | solution.py:21
  6.1 19.3 %collective-permute-start.3 = (f32[10,32,128]{2,1,0:T(8,128)S(1)}, f32[10,32,128]{2,1,0:T(8,128)S(1)}, u32[]{:S(2)}, u32[]{:S(2)}) collective-permute-start(f32[10,32,128]{2,1,0:T(8,128)S(1)} %get-tuple-element.41), channel_id=1, source_target_pairs={{0,16},{16,0},{1,17},{17,1},{2,18},{18,2},{3,19},{19,3},{4,20},{20... | collective-permute-start | bytes 491528 | tf_op jit(solution)/shard_map/ppermute | solution.py:21
  6.2 17.6 %collective-permute-start.2 = (f32[10,32,128]{2,1,0:T(8,128)S(1)}, f32[10,32,128]{2,1,0:T(8,128)S(1)}, u32[]{:S(2)}, u32[]{:S(2)}) collective-permute-start(f32[10,32,128]{2,1,0:T(8,128)S(1)} %get-tuple-element.42), channel_id=1, source_target_pairs={{0,16},{16,0},{1,17},{17,1},{2,18},{18,2},{3,19},{19,3},{4,20},{20... | collective-permute-start | bytes 491528 | tf_op jit(solution)/shard_map/ppermute | solution.py:21
  8.2 13.6 %collective-permute-start.1 = (f32[10,32,128]{2,1,0:T(8,128)S(1)}, f32[10,32,128]{2,1,0:T(8,128)S(1)}, u32[]{:S(2)}, u32[]{:S(2)}) collective-permute-start(f32[10,32,128]{2,1,0:T(8,128)S(1)} %get-tuple-element.43), channel_id=1, source_target_pairs={{0,16},{16,0},{1,17},{17,1},{2,18},{18,2},{3,19},{19,3},{4,20},{20... | collective-permute-start | bytes 491528 | tf_op jit(solution)/shard_map/ppermute | solution.py:21
  8.3 20.4 %collective-permute-start.9 = (f32[6,64,128]{2,1,0:T(8,128)S(1)}, f32[6,64,128]{2,1,0:T(8,128)S(1)}, u32[]{:S(2)}, u32[]{:S(2)}) collective-permute-start(f32[6,64,128]{2,1,0:T(8,128)S(1)} %get-tuple-element.38), channel_id=1, source_target_pairs={{0,16},{16,0},{1,17},{17,1},{2,18},{18,2},{3,19},{19,3},{4,20},{20... | collective-permute-start | bytes 589832 | tf_op jit(solution)/shard_map/ppermute | solution.py:21
  10.3 18.7 %copy-start.1 = (f32[256,64]{0,1:T(8,128)S(1)}, f32[256,64]{0,1:T(8,128)}, u32[]{:S(2)}) copy-start(f32[256,64]{0,1:T(8,128)} %param.9) | copy-start | bytes 196612
  10.3 18.7 %copy-start.2 = (f32[256]{0:T(256)S(1)}, f32[256]{0:T(256)}, u32[]{:S(2)}) copy-start(f32[256]{0:T(256)} %param.7) | copy-start | bytes 3076
  10.3 18.7 %copy-start.3 = (f32[256]{0:T(256)S(1)}, f32[256]{0:T(256)}, u32[]{:S(2)}) copy-start(f32[256]{0:T(256)} %param.8) | copy-start | bytes 3076
  21.7 15.6 %collective-permute-start = (f32[6,64,128]{2,1,0:T(8,128)S(1)}, f32[6,64,128]{2,1,0:T(8,128)S(1)}, u32[]{:S(2)}, u32[]{:S(2)}) collective-permute-start(f32[6,64,128]{2,1,0:T(8,128)S(1)} %get-tuple-element.39), channel_id=1, source_target_pairs={{0,16},{16,0},{1,17},{17,1},{2,18},{18,2},{3,19},{19,3},{4,20},{20... | collective-permute-start | bytes 589832 | tf_op jit(solution)/shard_map/ppermute | solution.py:21
  23.8 8.9 %collective-permute-start.11 = (f32[10,32,128]{2,1,0:T(8,128)S(1)}, f32[10,32,128]{2,1,0:T(8,128)S(1)}, u32[]{:S(2)}, u32[]{:S(2)}) collective-permute-start(f32[10,32,128]{2,1,0:T(8,128)S(1)} %slice_add_fusion.3.refs_3_), channel_id=1, source_target_pairs={{0,4},{4,8},{8,12},{12,0},{1,5},{5,9},{9,13},{13,1},{2,6},{6,10},{... | collective-permute-start | bytes 491528 | tf_op jit(solution)/shard_map/ppermute | solution.py:21
  25.4 10.9 %collective-permute-start.10 = (f32[10,32,128]{2,1,0:T(8,128)S(1)}, f32[10,32,128]{2,1,0:T(8,128)S(1)}, u32[]{:S(2)}, u32[]{:S(2)}) collective-permute-start(f32[10,32,128]{2,1,0:T(8,128)S(1)} %slice_add_fusion.refs_2_), channel_id=1, source_target_pairs={{0,4},{4,8},{8,12},{12,0},{1,5},{5,9},{9,13},{13,1},{2,6},{6,10},{... | collective-permute-start | bytes 491528 | tf_op jit(solution)/shard_map/ppermute | solution.py:21
  27.1 11.5 %collective-permute-start.6 = (f32[10,32,128]{2,1,0:T(8,128)S(1)}, f32[10,32,128]{2,1,0:T(8,128)S(1)}, u32[]{:S(2)}, u32[]{:S(2)}) collective-permute-start(f32[10,32,128]{2,1,0:T(8,128)S(1)} %slice_add_fusion.1.refs_3_), channel_id=1, source_target_pairs={{0,4},{4,8},{8,12},{12,0},{1,5},{5,9},{9,13},{13,1},{2,6},{6,10},{... | collective-permute-start | bytes 491528 | tf_op jit(solution)/shard_map/ppermute | solution.py:21
  28.7 12.0 %collective-permute-start.5 = (f32[10,32,128]{2,1,0:T(8,128)S(1)}, f32[10,32,128]{2,1,0:T(8,128)S(1)}, u32[]{:S(2)}, u32[]{:S(2)}) collective-permute-start(f32[10,32,128]{2,1,0:T(8,128)S(1)} %slice_add_fusion.2.refs_2_), channel_id=1, source_target_pairs={{0,4},{4,8},{8,12},{12,0},{1,5},{5,9},{9,13},{13,1},{2,6},{6,10},{... | collective-permute-start | bytes 491528 | tf_op jit(solution)/shard_map/ppermute | solution.py:21
  36.6 5.9 %collective-permute-start.12 = (f32[64,128]{1,0:T(8,128)S(1)}, f32[64,128]{1,0:T(8,128)S(1)}, u32[]{:S(2)}, u32[]{:S(2)}) collective-permute-start(f32[64,128]{1,0:T(8,128)S(1)} %get-tuple-element.29), channel_id=1, source_target_pairs={{0,8},{4,12},{8,0},{12,4},{1,9},{5,13},{9,1},{13,5},{2,10},{6,14},... | collective-permute-start | bytes 98312 | tf_op jit(solution)/shard_map/ppermute | solution.py:25
  40.9 4.9 %collective-permute-start.7 = (f32[64,128]{1,0:T(8,128)S(1)}, f32[64,128]{1,0:T(8,128)S(1)}, u32[]{:S(2)}, u32[]{:S(2)}) collective-permute-start(f32[64,128]{1,0:T(8,128)S(1)} %get-tuple-element.26), channel_id=1, source_target_pairs={{0,8},{4,12},{8,0},{12,4},{1,9},{5,13},{9,1},{13,5},{2,10},{6,14},... | collective-permute-start | bytes 98312 | tf_op jit(solution)/shard_map/ppermute | solution.py:25
  42.5 4.0 %collective-permute-start.13 = (f32[64,128]{1,0:T(8,128)S(1)}, f32[64,128]{1,0:T(8,128)S(1)}, u32[]{:S(2)}, u32[]{:S(2)}) collective-permute-start(f32[64,128]{1,0:T(8,128)S(1)} %shard_map.73), channel_id=1, source_target_pairs={{0,4},{4,0},{8,12},{12,8},{1,5},{5,1},{9,13},{13,9},{2,6},{6,2},{1... | collective-permute-start | bytes 98312 | tf_op jit(solution)/shard_map/ppermute | solution.py:25
  45.8 4.0 %collective-permute-start.8 = (f32[64,128]{1,0:T(8,128)S(1)}, f32[64,128]{1,0:T(8,128)S(1)}, u32[]{:S(2)}, u32[]{:S(2)}) collective-permute-start(f32[64,128]{1,0:T(8,128)S(1)} %shard_map.70), channel_id=1, source_target_pairs={{0,4},{4,0},{8,12},{12,8},{1,5},{5,1},{9,13},{13,9},{2,6},{6,2},{1... | collective-permute-start | bytes 98312 | tf_op jit(solution)/shard_map/ppermute | solution.py:25

commit v5 on v4

--- a/solution.py
+++ b/solution.py
@@ -132,16 +132,6 @@
     each_block(begin, pieces, refs, use)
 
 
-def exposure_kernel(begin, pieces, *refs):
-    dates_dev = refs[0].shape[0]
-
-    def use(at, size, rows, found):
-        for t, exposure in enumerate(found):
-            refs[-1][pl.ds(at * dates_dev + t, size, stride=dates_dev), :] = exposure
-
-    each_block(begin, pieces, refs, use)
-
-
 def entering(stages, others, coef_ref, inside, rows):
     mine, count = lax.axis_index("date"), lax.axis_size("date")
     arrived = jnp.where(mine >= count // 2, others[0][inside, :], 0.0)
@@ -160,31 +150,72 @@
     refs[-1][...] = jnp.where(upper, arrived, longer)
 
 
-def funding_kernel(begin, stages, *refs):
-    coef_ref, cost_ref, rate_ref, net_ref = refs[stages : stages + 4]
-    net_out, out, held_ref, sem = refs[-4:]
-    dates_dev, size = cost_ref.shape[:2]
+def accumulate(begin, size, others, coef_ref, cost_ref, rate_ref, out, held_ref, sem):
+    dates_dev = rate_ref.shape[0]
     block = LEAVING * dates_dev
-
-    def leaving(part):
-        here, there = pl.ds(part * block, block), pl.ds(begin * dates_dev + part * block, block)
-        return pltpu.make_async_copy(held_ref.at[here, :], out.at[there, :], sem.at[part + 1])
-
-    there = pl.ds(begin * dates_dev, size * dates_dev)
-    exposed = pltpu.make_async_copy(net_ref, net_out.at[there, :], sem.at[0])
-    exposed.start()
-    parts = range(size // LEAVING)
-    for part in parts:
-        inside = pl.ds(part * LEAVING, LEAVING)
-        rows = pl.ds(begin + part * LEAVING, LEAVING)
-        state = entering(stages, refs[:stages], coef_ref, inside, rows)
+    copies = []
+    for part in range(size // LEAVING):
+        low = begin + part * LEAVING
+        inside, rows = pl.ds(part * LEAVING, LEAVING), pl.ds(low, LEAVING)
+        if others:
+            state = entering(len(others), others, coef_ref, inside, rows)
+        else:
+            state = jnp.zeros_like(coef_ref[0, rows, :])
         for t in range(dates_dev):
             state = rate_ref[t, rows, :] * state + cost_ref[t, inside, :]
-            held_ref[pl.ds(part * block + t, LEAVING, stride=dates_dev), :] = state
-        leaving(part).start()
-    exposed.wait()
-    for part in parts:
-        leaving(part).wait()
+            held_ref[pl.ds(low * dates_dev + t, LEAVING, stride=dates_dev), :] = state
+        here = pl.ds(low * dates_dev, block)
+        copies.append(pltpu.make_async_copy(held_ref.at[here, :], out.at[here, :], sem.at[low // LEAVING]))
+        copies[-1].start()
+    return copies
+
+
+def settle_kernel(groups, stages, *refs):
+    refs = list(refs)
+    net_out, out, net_ref, held_ref, net_sem, sem = refs[-6:]
+    own_ref, level_ref, coef_ref, rate_ref = refs[:4]
+    cost_refs = refs[4 : 4 + len(groups)]
+    at = 4 + len(groups)
+    dates_dev = rate_ref.shape[0]
+    arrived = []
+    for _ in groups[:-1]:
+        arrived.append(refs[at : at + stages])
+        at += stages
+    copies = []
+    for low, high, mine in groups:
+        count = 1 + 2 * len(mine)
+        parts = [own_ref, *refs[at : at + count], level_ref]
+        at += count
+
+        def use(row, size, rows, found, low=low):
+            for t, exposure in enumerate(found):
+                net_ref[pl.ds((low + row) * dates_dev + t, size, stride=dates_dev), :] = exposure
+            here = pl.ds((low + row) * dates_dev, size * dates_dev)
+            copies.append(pltpu.make_async_copy(net_ref.at[here, :], net_out.at[here, :], net_sem.at[len(copies)]))
+            copies[-1].start()
+
+        each_block(low, len(mine), parts, use)
+    for (low, high, _), cost_ref, others in zip(groups, cost_refs, arrived):
+        copies += accumulate(low, high - low, others, coef_ref, cost_ref, rate_ref, out, held_ref, sem)
+
+    @pl.when(lax.axis_index("date") == 0)
+    def _():
+        low, high, _ = groups[-1]
+        for copy in accumulate(low, high - low, (), coef_ref, cost_refs[-1], rate_ref, out, held_ref, sem):
+            copy.wait()
+
+    for copy in copies:
+        copy.wait()
+
+
+def funding_kernel(low, high, stages, *refs):
+    coef_ref, cost_ref, rate_ref = refs[stages : stages + 3]
+    out, held_ref, sem = refs[-3:]
+
+    @pl.when(lax.axis_index("date") != 0)
+    def _():
+        for copy in accumulate(low, high - low, refs[:stages], coef_ref, cost_ref, rate_ref, out, held_ref, sem):
+            copy.wait()
 
 
 def shards(trade_values, set_of_trade, thresholds, spreads, retention):
@@ -228,32 +259,43 @@
     )
 
     flat = (sets * dates_dev, paths)
-    results = ()
+    costs, arrived, inputs = [], [], []
     for g, (low, high, mine) in enumerate(groups):
         size = high - low
-        parts = (own, other[g], *[late[k] for k in mine], *[rims[k] for k in mine])
-        costs, last, sent = call(
+        parts = (other[g], *[late[k] for k in mine], *[rims[k] for k in mine])
+        inputs += parts
+        cost, last, sent = call(
             functools.partial(cost_kernel, low, len(mine)),
-            (*parts, level_all, spread_all, rate_all, coefs),
+            (own, *parts, level_all, spread_all, rate_all, coefs),
             ((dates_dev, size, paths), (size, paths), (size, paths)),
         )
-        (exposed,) = call(
-            functools.partial(exposure_kernel, low, len(mine)), (*parts, level_all), ((size * dates_dev, paths),)
-        )
+        costs.append(cost)
         others = []
         for stage in range(stages):
             if stage:
                 (sent,) = call(functools.partial(join_kernel, low, stage), (last, coefs, *others), ((size, paths),))
             others.append(exchanged(sent, "date", count >> (stage + 1)))
-        results = call(
-            functools.partial(funding_kernel, low, stages),
-            (*others, coefs, costs, rate_all, exposed),
-            (flat, flat),
-            [pltpu.VMEM((size * dates_dev, paths), jnp.float32), pltpu.SemaphoreType.DMA((1 + size // LEAVING,))],
-            True,
-            results,
-        )
-    return tuple(result.reshape(sets, dates_dev, paths) for result in results)
+        arrived.append(others)
+
+    held, leaving = pltpu.VMEM(flat, jnp.float32), pltpu.SemaphoreType.DMA((sets // LEAVING,))
+    early_carries = [part for others in arrived[:-1] for part in others]
+    net_exposure, funding = call(
+        functools.partial(settle_kernel, groups, stages),
+        (own, level_all, coefs, rate_all, *costs, *early_carries, *inputs),
+        (flat, flat),
+        [held, held, leaving, leaving],
+        True,
+    )
+    low, high, _ = groups[-1]
+    (funding,) = call(
+        functools.partial(funding_kernel, low, high, stages),
+        (*arrived[-1], coefs, costs[-1], rate_all),
+        (flat,),
+        [held, leaving],
+        True,
+        (funding,),
+    )
+    return tuple(result.reshape(sets, dates_dev, paths) for result in (net_exposure, funding))
 
 
 def solution(mesh):

time: 51 us -> 50.1 us (0.982)
  waiting for transfers between devices: 26.1 us -> 24.3 us
  starting transfers between devices: 17.1 us -> 18.6 us
  Pallas kernels: 3.72 us -> 3.13 us
    ppermute x10, starting transfers between devices: 14.3 us -> 15.8 us  [ahead(): lax.ppermute(value, axis, [(i, (i + 1) % count) for i in range(count)])]
    ppermute x10, waiting for transfers between devices: 20.9 us -> 19.4 us  [ahead(): lax.ppermute(value, axis, [(i, (i + 1) % count) for i in range(count)])]
    pallas_call x9 -> x7, Pallas kernels: 3.72 us -> 3.13 us  [call(): pl.pallas_call(body, out_shape=[jax.ShapeDtypeStruct(s, jnp.float32) for...]
  transfers between devices with their start and end apart: 14 -> 14, of which waited for: 7 -> 9; matrix products, arithmetic and copies ran while one was open for 1% -> 2% of each run, Pallas kernels for 5% -> 6%
where the time goes in v5:
time: 50.1 us; the launch traced here: 50 us
  waiting for transfers between devices  24.3 us (49%)
  starting transfers between devices  18.6 us (37%)
  Pallas kernels  3.13 us (6%)
  matrix products  1.25 us (2%)
  local copies, waits for them, and re-layouts  0.99 us (2%)
  other arithmetic  0.95 us (2%)
  between operations  0.75 us (1%)
    ppermute x10, waiting for transfers between devices, ahead(): lax.ppermute(value, axis, [(i, (i + 1) % count) for i in range(count)])  19.4 us
    ppermute x10, starting transfers between devices, ahead(): lax.ppermute(value, axis, [(i, (i + 1) % count) for i in range(count)])  15.8 us
    ppermute x4, waiting for transfers between devices, exchanged(): lax.ppermute(value, axis, [(i, i ^ bit) for i in range(lax.axis_size(axis...  4.89 us
    pallas_call x7, Pallas kernels, call(): pl.pallas_call(body, out_shape=[jax.ShapeDtypeStruct(s, jnp.float32) for...  3.13 us
    ppermute x4, starting transfers between devices, exchanged(): lax.ppermute(value, axis, [(i, i ^ bit) for i in range(lax.axis_size(axis...  2.82 us
    dot_general x2, matrix products, row_sums(): jnp.einsum('sn,ntp->tsp', selector, values, preferred_element_type=jnp.fl...  1.25 us
  transfers between devices with their start and end apart: 14, of which 9 were waited for; matrix products, arithmetic and copies ran while one was open for 2% of the time, Pallas kernels for 6%

profile of v5, /device:TPU:0, one launch (start us, length us, event | category | flops | bytes accessed | tf_op | source)
XLA Modules:
  0.0 50.0 jit_solution(12878240219443200866)
XLA Ops:
  0.6 0.8 %broadcast_add_fusion = (s32[640]{0:T(1024)S(1)}, s32[640]{0:T(1024)S(1)}) fusion(s32[640]{0:T(1024)} %param.6, s32[]{:T(128)S(6)} %mul.3), kind=kLoop, calls=%fused_computation.17 | loop fusion | flops 3200 | bytes 7684 | tf_op jit(solution)/shard_map/sub | solution.py:237
  1.5 0.9 %copy-done = bf16[640,16,128]{2,1,0:T(8,128)(2,1)S(1)} copy-done((bf16[640,16,128]{2,1,0:T(8,128)(2,1)S(1)}, bf16[640,16,128]{2,1,0:T(8,128)(2,1)}, u32[]{:S(2)}) %copy-start) | copy-done | bytes 2621464
  2.4 0.6 %fusion.7 = f32[16,128,128]{2,1,0:T(8,128)S(1)} fusion(bf16[640,16,128]{2,1,0:T(8,128)(2,1)S(1)} %copy-done, s32[640]{0:T(1024)S(1)} %get-tuple-element.32), kind=kOutput, calls=%fused_computation.5 | convolution fusion | flops 335626240 | bytes 3672576 | tf_op jit(solution)/shard_map/sn,ntp->tsp/dot_general | solution.py:31
  3.1 3.1 %collective-permute-start.7 = (f32[10,32,128]{2,1,0:T(8,128)S(1)}, f32[10,32,128]{2,1,0:T(8,128)S(1)}, u32[]{:S(2)}, u32[]{:S(2)}) collective-permute-start(f32[10,32,128]{2,1,0:T(8,128)S(1)} %get-tuple-element.34), channel_id=1, source_target_pairs={{0,16},{16,0},{1,17},{17,1},{2,18},{18,2},{3,19},{19,3},{4,20},{20... | collective-permute-start | bytes 491528 | tf_op jit(solution)/shard_map/ppermute | solution.py:21
  6.2 1.9 %collective-permute-start.2 = (f32[10,32,128]{2,1,0:T(8,128)S(1)}, f32[10,32,128]{2,1,0:T(8,128)S(1)}, u32[]{:S(2)}, u32[]{:S(2)}) collective-permute-start(f32[10,32,128]{2,1,0:T(8,128)S(1)} %get-tuple-element.36), channel_id=1, source_target_pairs={{0,16},{16,0},{1,17},{17,1},{2,18},{18,2},{3,19},{19,3},{4,20},{20... | collective-permute-start | bytes 491528 | tf_op jit(solution)/shard_map/ppermute | solution.py:21
  8.3 2.0 %collective-permute-start.5 = (f32[6,64,128]{2,1,0:T(8,128)S(1)}, f32[6,64,128]{2,1,0:T(8,128)S(1)}, u32[]{:S(2)}, u32[]{:S(2)}) collective-permute-start(f32[6,64,128]{2,1,0:T(8,128)S(1)} %get-tuple-element.38), channel_id=1, source_target_pairs={{0,16},{16,0},{1,17},{17,1},{2,18},{18,2},{3,19},{19,3},{4,20},{20... | collective-permute-start | bytes 589832 | tf_op jit(solution)/shard_map/ppermute | solution.py:21
  10.3 0.6 %fusion.4.refs_0_ = f32[16,128,128]{2,1,0:T(8,128)S(1)} fusion(bf16[640,16,128]{2,1,0:T(8,128)(2,1)S(1)} %copy-done, s32[640]{0:T(1024)S(1)} %get-tuple-element.33), kind=kOutput, calls=%fused_computation.4 | convolution fusion | flops 335626240 | bytes 3672576 | tf_op jit(solution)/shard_map/sn,ntp->tsp/dot_general | solution.py:31
  10.9 10.8 %collective-permute-done.1 = f32[10,32,128]{2,1,0:T(8,128)S(1)} collective-permute-done((f32[10,32,128]{2,1,0:T(8,128)S(1)}, f32[10,32,128]{2,1,0:T(8,128)S(1)}, u32[]{:S(2)}, u32[]{:S(2)}) %collective-permute-start.1) | collective-permute-done | bytes 163872 | tf_op jit(solution)/shard_map/ppermute | solution.py:21
  21.7 2.0 %collective-permute-start = (f32[6,64,128]{2,1,0:T(8,128)S(1)}, f32[6,64,128]{2,1,0:T(8,128)S(1)}, u32[]{:S(2)}, u32[]{:S(2)}) collective-permute-start(f32[6,64,128]{2,1,0:T(8,128)S(1)} %get-tuple-element.39), channel_id=1, source_target_pairs={{0,16},{16,0},{1,17},{17,1},{2,18},{18,2},{3,19},{19,3},{4,20},{20... | collective-permute-start | bytes 589832 | tf_op jit(solution)/shard_map/ppermute | solution.py:21
  23.8 1.6 %collective-permute-start.4 = (f32[10,32,128]{2,1,0:T(8,128)S(1)}, f32[10,32,128]{2,1,0:T(8,128)S(1)}, u32[]{:S(2)}, u32[]{:S(2)}) collective-permute-start(f32[10,32,128]{2,1,0:T(8,128)S(1)} %slice_add_fusion.3.refs_3_.refs_10_), channel_id=1, source_target_pairs={{0,4},{4,8},{8,12},{12,0},{1,5},{5,9},{9,13},{13,1},{2,6},{6,10},{... | collective-permute-start | bytes 491528 | tf_op jit(solution)/shard_map/ppermute | solution.py:21
  25.4 1.6 %collective-permute-start.3 = (f32[10,32,128]{2,1,0:T(8,128)S(1)}, f32[10,32,128]{2,1,0:T(8,128)S(1)}, u32[]{:S(2)}, u32[]{:S(2)}) collective-permute-start(f32[10,32,128]{2,1,0:T(8,128)S(1)} %slice_add_fusion.refs_2_.refs_9_), channel_id=1, source_target_pairs={{0,4},{4,8},{8,12},{12,0},{1,5},{5,9},{9,13},{13,1},{2,6},{6,10},{... | collective-permute-start | bytes 491528 | tf_op jit(solution)/shard_map/ppermute | solution.py:21
  27.1 1.6 %collective-permute-start.9 = (f32[10,32,128]{2,1,0:T(8,128)S(1)}, f32[10,32,128]{2,1,0:T(8,128)S(1)}, u32[]{:S(2)}, u32[]{:S(2)}) collective-permute-start(f32[10,32,128]{2,1,0:T(8,128)S(1)} %slice_add_fusion.1.refs_3_.refs_15_), channel_id=1, source_target_pairs={{0,4},{4,8},{8,12},{12,0},{1,5},{5,9},{9,13},{13,1},{2,6},{6,10},{... | collective-permute-start | bytes 491528 | tf_op jit(solution)/shard_map/ppermute | solution.py:21
  28.7 0.6 %collective-permute-done.refs_1_.refs_8_ = f32[6,64,128]{2,1,0:T(8,128)S(1)} collective-permute-done((f32[6,64,128]{2,1,0:T(8,128)S(1)}, f32[6,64,128]{2,1,0:T(8,128)S(1)}, u32[]{:S(2)}, u32[]{:S(2)}) %collective-permute-start) | collective-permute-done | bytes 196640 | tf_op jit(solution)/shard_map/ppermute | solution.py:21
  29.3 1.8 %collective-permute-start.8 = (f32[10,32,128]{2,1,0:T(8,128)S(1)}, f32[10,32,128]{2,1,0:T(8,128)S(1)}, u32[]{:S(2)}, u32[]{:S(2)}) collective-permute-start(f32[10,32,128]{2,1,0:T(8,128)S(1)} %slice_add_fusion.2.refs_2_.refs_14_), channel_id=1, source_target_pairs={{0,4},{4,8},{8,12},{12,0},{1,5},{5,9},{9,13},{13,1},{2,6},{6,10},{... | collective-permute-start | bytes 491528 | tf_op jit(solution)/shard_map/ppermute | solution.py:21
  31.1 0.7 %shard_map.68 = (f32[16,128,128]{2,1,0:T(8,128)S(1)}, f32[128,128]{1,0:T(8,128)S(1)}, f32[128,128]{1,0:T(8,128)S(1)}, f32[4,128,128]{2,1,0:T(8,128)S(1)}) custom-call(f32[64,256]{1,0:T(8,128)S(1)} %bitcast.15, f32[2,128]{1,0:T(2,128)S(1)} %bitcast.16, f32[2,128]{1,0:T(2,128)S(1)} %bitcast.17), custom_call_target="tpu_custom_call" | custom-call | flops 417792 | bytes 208896 | tf_op jit(solution)/shard_map/pallas_call | solution.py:44
  31.8 1.0 %collective-permute-done.4.refs_5_.refs_12_ = f32[10,32,128]{2,1,0:T(8,128)S(1)} collective-permute-done((f32[10,32,128]{2,1,0:T(8,128)S(1)}, f32[10,32,128]{2,1,0:T(8,128)S(1)}, u32[]{:S(2)}, u32[]{:S(2)}) %collective-permute-start.4) | collective-permute-done | bytes 163872 | tf_op jit(solution)/shard_map/ppermute | solution.py:21
  32.7 3.6 %collective-permute-done.3.refs_4_.refs_11_ = f32[10,32,128]{2,1,0:T(8,128)S(1)} collective-permute-done((f32[10,32,128]{2,1,0:T(8,128)S(1)}, f32[10,32,128]{2,1,0:T(8,128)S(1)}, u32[]{:S(2)}, u32[]{:S(2)}) %collective-permute-start.3) | collective-permute-done | bytes 163872 | tf_op jit(solution)/shard_map/ppermute | solution.py:21
  36.6 0.8 %collective-permute-start.10 = (f32[64,128]{1,0:T(8,128)S(1)}, f32[64,128]{1,0:T(8,128)S(1)}, u32[]{:S(2)}, u32[]{:S(2)}) collective-permute-start(f32[64,128]{1,0:T(8,128)S(1)} %get-tuple-element.26), channel_id=1, source_target_pairs={{0,8},{4,12},{8,0},{12,4},{1,9},{5,13},{9,1},{13,5},{2,10},{6,14},... | collective-permute-start | bytes 98312 | tf_op jit(solution)/shard_map/ppermute | solution.py:25
  37.3 1.3 %collective-permute-done.9.refs_5_.refs_17_ = f32[10,32,128]{2,1,0:T(8,128)S(1)} collective-permute-done((f32[10,32,128]{2,1,0:T(8,128)S(1)}, f32[10,32,128]{2,1,0:T(8,128)S(1)}, u32[]{:S(2)}, u32[]{:S(2)}) %collective-permute-start.9) | collective-permute-done | bytes 163872 | tf_op jit(solution)/shard_map/ppermute | solution.py:21
  38.6 2.1 %collective-permute-done.8.refs_4_.refs_16_ = f32[10,32,128]{2,1,0:T(8,128)S(1)} collective-permute-done((f32[10,32,128]{2,1,0:T(8,128)S(1)}, f32[10,32,128]{2,1,0:T(8,128)S(1)}, u32[]{:S(2)}, u32[]{:S(2)}) %collective-permute-start.8) | collective-permute-done | bytes 163872 | tf_op jit(solution)/shard_map/ppermute | solution.py:21
  40.9 1.5 %collective-permute-start.12 = (f32[64,128]{1,0:T(8,128)S(1)}, f32[64,128]{1,0:T(8,128)S(1)}, u32[]{:S(2)}, u32[]{:S(2)}) collective-permute-start(f32[64,128]{1,0:T(8,128)S(1)} %get-tuple-element.29), channel_id=1, source_target_pairs={{0,8},{4,12},{8,0},{12,4},{1,9},{5,13},{9,1},{13,5},{2,10},{6,14},... | collective-permute-start | bytes 98312 | tf_op jit(solution)/shard_map/ppermute | solution.py:25
  43.0 2.9 %collective-permute-done.12.refs_0_ = f32[64,128]{1,0:T(8,128)S(1)} collective-permute-done((f32[64,128]{1,0:T(8,128)S(1)}, f32[64,128]{1,0:T(8,128)S(1)}, u32[]{:S(2)}, u32[]{:S(2)}) %collective-permute-start.12) | collective-permute-done | bytes 32800 | tf_op jit(solution)/shard_map/ppermute | solution.py:25
  46.4 1.9 %shard_map.72 = (f32[2048,128]{1,0:T(8,128)}, f32[2048,128]{1,0:T(8,128)}) custom-call(f32[16,128,128]{2,1,0:T(8,128)S(1)} %fusion.4.refs_0_, f32[128,128]{1,0:T(8,128)S(1)} %get-tuple-element.17.refs_6_.refs_1_, f32[4,128,128]{2,1,0:T(8,128)S(1)} %get-tuple-element.18.refs_9_.coef_ref.refs_2_, ...), custom_call_target="tpu_custom_call" | custom-call | flops 14680064 | bytes 7340032 | tf_op jit(solution)/shard_map/pallas_call | solution.py:44
  48.3 1.5 %collective-permute-done.13.refs_1_ = f32[64,128]{1,0:T(8,128)S(1)} collective-permute-done((f32[64,128]{1,0:T(8,128)S(1)}, f32[64,128]{1,0:T(8,128)S(1)}, u32[]{:S(2)}, u32[]{:S(2)}) %collective-permute-start.13) | collective-permute-done | bytes 32800 | tf_op jit(solution)/shard_map/ppermute | solution.py:25
  (28 shorter events, 2.0 us)
Async XLA Ops:
  0.6 1.8 %copy-start = (bf16[640,16,128]{2,1,0:T(8,128)(2,1)S(1)}, bf16[640,16,128]{2,1,0:T(8,128)(2,1)}, u32[]{:S(2)}) copy-start(bf16[640,16,128]{2,1,0:T(8,128)(2,1)} %param.5) | copy-start | bytes 7864324
  3.1 24.0 %collective-permute-start.7 = (f32[10,32,128]{2,1,0:T(8,128)S(1)}, f32[10,32,128]{2,1,0:T(8,128)S(1)}, u32[]{:S(2)}, u32[]{:S(2)}) collective-permute-start(f32[10,32,128]{2,1,0:T(8,128)S(1)} %get-tuple-element.34), channel_id=1, source_target_pairs={{0,16},{16,0},{1,17},{17,1},{2,18},{18,2},{3,19},{19,3},{4,20},{20... | collective-permute-start | bytes 491528 | tf_op jit(solution)/shard_map/ppermute | solution.py:21
  6.1 19.3 %collective-permute-start.6 = (f32[10,32,128]{2,1,0:T(8,128)S(1)}, f32[10,32,128]{2,1,0:T(8,128)S(1)}, u32[]{:S(2)}, u32[]{:S(2)}) collective-permute-start(f32[10,32,128]{2,1,0:T(8,128)S(1)} %get-tuple-element.35), channel_id=1, source_target_pairs={{0,16},{16,0},{1,17},{17,1},{2,18},{18,2},{3,19},{19,3},{4,20},{20... | collective-permute-start | bytes 491528 | tf_op jit(solution)/shard_map/ppermute | solution.py:21
  6.2 17.6 %collective-permute-start.2 = (f32[10,32,128]{2,1,0:T(8,128)S(1)}, f32[10,32,128]{2,1,0:T(8,128)S(1)}, u32[]{:S(2)}, u32[]{:S(2)}) collective-permute-start(f32[10,32,128]{2,1,0:T(8,128)S(1)} %get-tuple-element.36), channel_id=1, source_target_pairs={{0,16},{16,0},{1,17},{17,1},{2,18},{18,2},{3,19},{19,3},{4,20},{20... | collective-permute-start | bytes 491528 | tf_op jit(solution)/shard_map/ppermute | solution.py:21
  8.2 13.6 %collective-permute-start.1 = (f32[10,32,128]{2,1,0:T(8,128)S(1)}, f32[10,32,128]{2,1,0:T(8,128)S(1)}, u32[]{:S(2)}, u32[]{:S(2)}) collective-permute-start(f32[10,32,128]{2,1,0:T(8,128)S(1)} %get-tuple-element.37), channel_id=1, source_target_pairs={{0,16},{16,0},{1,17},{17,1},{2,18},{18,2},{3,19},{19,3},{4,20},{20... | collective-permute-start | bytes 491528 | tf_op jit(solution)/shard_map/ppermute | solution.py:21
  8.3 29.0 %collective-permute-start.5 = (f32[6,64,128]{2,1,0:T(8,128)S(1)}, f32[6,64,128]{2,1,0:T(8,128)S(1)}, u32[]{:S(2)}, u32[]{:S(2)}) collective-permute-start(f32[6,64,128]{2,1,0:T(8,128)S(1)} %get-tuple-element.38), channel_id=1, source_target_pairs={{0,16},{16,0},{1,17},{17,1},{2,18},{18,2},{3,19},{19,3},{4,20},{20... | collective-permute-start | bytes 589832 | tf_op jit(solution)/shard_map/ppermute | solution.py:21
  10.3 20.8 %copy-start.1 = (f32[256,64]{0,1:T(8,128)S(1)}, f32[256,64]{0,1:T(8,128)}, u32[]{:S(2)}) copy-start(f32[256,64]{0,1:T(8,128)} %param.9) | copy-start | bytes 196612
  10.3 20.8 %copy-start.2 = (f32[256]{0:T(256)S(1)}, f32[256]{0:T(256)}, u32[]{:S(2)}) copy-start(f32[256]{0:T(256)} %param.7) | copy-start | bytes 3076
  10.3 20.8 %copy-start.3 = (f32[256]{0:T(256)S(1)}, f32[256]{0:T(256)}, u32[]{:S(2)}) copy-start(f32[256]{0:T(256)} %param.8) | copy-start | bytes 3076
  21.7 7.6 %collective-permute-start = (f32[6,64,128]{2,1,0:T(8,128)S(1)}, f32[6,64,128]{2,1,0:T(8,128)S(1)}, u32[]{:S(2)}, u32[]{:S(2)}) collective-permute-start(f32[6,64,128]{2,1,0:T(8,128)S(1)} %get-tuple-element.39), channel_id=1, source_target_pairs={{0,16},{16,0},{1,17},{17,1},{2,18},{18,2},{3,19},{19,3},{4,20},{20... | collective-permute-start | bytes 589832 | tf_op jit(solution)/shard_map/ppermute | solution.py:21
  23.8 8.9 %collective-permute-start.4 = (f32[10,32,128]{2,1,0:T(8,128)S(1)}, f32[10,32,128]{2,1,0:T(8,128)S(1)}, u32[]{:S(2)}, u32[]{:S(2)}) collective-permute-start(f32[10,32,128]{2,1,0:T(8,128)S(1)} %slice_add_fusion.3.refs_3_.refs_10_), channel_id=1, source_target_pairs={{0,4},{4,8},{8,12},{12,0},{1,5},{5,9},{9,13},{13,1},{2,6},{6,10},{... | collective-permute-start | bytes 491528 | tf_op jit(solution)/shard_map/ppermute | solution.py:21
  25.4 10.9 %collective-permute-start.3 = (f32[10,32,128]{2,1,0:T(8,128)S(1)}, f32[10,32,128]{2,1,0:T(8,128)S(1)}, u32[]{:S(2)}, u32[]{:S(2)}) collective-permute-start(f32[10,32,128]{2,1,0:T(8,128)S(1)} %slice_add_fusion.refs_2_.refs_9_), channel_id=1, source_target_pairs={{0,4},{4,8},{8,12},{12,0},{1,5},{5,9},{9,13},{13,1},{2,6},{6,10},{... | collective-permute-start | bytes 491528 | tf_op jit(solution)/shard_map/ppermute | solution.py:21
  27.1 11.5 %collective-permute-start.9 = (f32[10,32,128]{2,1,0:T(8,128)S(1)}, f32[10,32,128]{2,1,0:T(8,128)S(1)}, u32[]{:S(2)}, u32[]{:S(2)}) collective-permute-start(f32[10,32,128]{2,1,0:T(8,128)S(1)} %slice_add_fusion.1.refs_3_.refs_15_), channel_id=1, source_target_pairs={{0,4},{4,8},{8,12},{12,0},{1,5},{5,9},{9,13},{13,1},{2,6},{6,10},{... | collective-permute-start | bytes 491528 | tf_op jit(solution)/shard_map/ppermute | solution.py:21
  29.3 11.4 %collective-permute-start.8 = (f32[10,32,128]{2,1,0:T(8,128)S(1)}, f32[10,32,128]{2,1,0:T(8,128)S(1)}, u32[]{:S(2)}, u32[]{:S(2)}) collective-permute-start(f32[10,32,128]{2,1,0:T(8,128)S(1)} %slice_add_fusion.2.refs_2_.refs_14_), channel_id=1, source_target_pairs={{0,4},{4,8},{8,12},{12,0},{1,5},{5,9},{9,13},{13,1},{2,6},{6,10},{... | collective-permute-start | bytes 491528 | tf_op jit(solution)/shard_map/ppermute | solution.py:21
  36.6 5.9 %collective-permute-start.10 = (f32[64,128]{1,0:T(8,128)S(1)}, f32[64,128]{1,0:T(8,128)S(1)}, u32[]{:S(2)}, u32[]{:S(2)}) collective-permute-start(f32[64,128]{1,0:T(8,128)S(1)} %get-tuple-element.26), channel_id=1, source_target_pairs={{0,8},{4,12},{8,0},{12,4},{1,9},{5,13},{9,1},{13,5},{2,10},{6,14},... | collective-permute-start | bytes 98312 | tf_op jit(solution)/shard_map/ppermute | solution.py:25
  40.9 4.9 %collective-permute-start.12 = (f32[64,128]{1,0:T(8,128)S(1)}, f32[64,128]{1,0:T(8,128)S(1)}, u32[]{:S(2)}, u32[]{:S(2)}) collective-permute-start(f32[64,128]{1,0:T(8,128)S(1)} %get-tuple-element.29), channel_id=1, source_target_pairs={{0,8},{4,12},{8,0},{12,4},{1,9},{5,13},{9,1},{13,5},{2,10},{6,14},... | collective-permute-start | bytes 98312 | tf_op jit(solution)/shard_map/ppermute | solution.py:25
  42.5 4.0 %collective-permute-start.11 = (f32[64,128]{1,0:T(8,128)S(1)}, f32[64,128]{1,0:T(8,128)S(1)}, u32[]{:S(2)}, u32[]{:S(2)}) collective-permute-start(f32[64,128]{1,0:T(8,128)S(1)} %shard_map.71), channel_id=1, source_target_pairs={{0,4},{4,0},{8,12},{12,8},{1,5},{5,1},{9,13},{13,9},{2,6},{6,2},{1... | collective-permute-start | bytes 98312 | tf_op jit(solution)/shard_map/ppermute | solution.py:25
  45.8 4.0 %collective-permute-start.13 = (f32[64,128]{1,0:T(8,128)S(1)}, f32[64,128]{1,0:T(8,128)S(1)}, u32[]{:S(2)}, u32[]{:S(2)}) collective-permute-start(f32[64,128]{1,0:T(8,128)S(1)} %shard_map.73), channel_id=1, source_target_pairs={{0,4},{4,0},{8,12},{12,8},{1,5},{5,1},{9,13},{13,9},{2,6},{6,2},{1... | collective-permute-start | bytes 98312 | tf_op jit(solution)/shard_map/ppermute | solution.py:25
